TPU v7x, 128 devices: a whole 4x4x4 slice. The times are simulated.
128 devices in a mesh: layer: 4 (over x), row: 16 (over z, y), col: 2 (over core).
Axes of the slice: x: 4, y: 4, z: 4, core: 2. Of those that a mesh axis runs over, the one named last changes fastest.
Arguments:
- density: bfloat16 [8192, 8192], P('row', 'col'), may hold values from -0.5 to 1.5
- pattern: int32 [64, 64], P('row', 'col'), may hold values from 0 to 1, as said below
- holder: int32 [4096, 1], P(('layer', 'row', 'col')), may hold values from 0 to 31; in each aligned block of 32 rows (0 to 31, 32 to 63, ...) at most 2 rows name the same one
- slot_index: int32 [4096], P(('layer', 'row', 'col')), may hold values from 0 to 31
- atom_index: int32 [4096], P(('layer', 'row', 'col')), may hold values from 0 to 7
- derivative: bfloat16 [4096, 3, 128, 128], P(('layer', 'row', 'col')), may hold values from -1.1953125 to 1.1953125
Outputs:
- forces: float32 [3, 1024], P(None, ('layer', 'row', 'col'))
Inputs may be any that keep to these rules, and one draw needn't show every extreme that they name: `pattern`: the blocks held by one (row, col) grid position form a tile of 4 x 32; in some tile every block is 1. Among the derivative blocks of one device no holder is named more than 2 times, a bound that some block reaches; every holder is named on some device.
All inputs are finite; a program needn't handle non-finite values.
Results may differ from a plain program's by a relative error of at most 0.015.
Values may be sent and summed in bfloat16 or wider, within the bound.
A program may use at most 128 MiB of HBM per device.

v0:
```python
import jax
import jax.numpy as jnp
from jax import lax
from jax.sharding import PartitionSpec as P

BS = 128
ATOM_DEV = 8


def in_order(parts, dim):
    parts = jnp.moveaxis(parts, 0, dim)
    shape = parts.shape
    return parts.reshape(*shape[:dim], shape[dim] * shape[dim + 1], *shape[dim + 2 :])


def copy_for_each(value, axis):
    length = lax.axis_size(axis)
    return lax.all_to_all(
        jnp.broadcast_to(value[None], (length, *value.shape)), axis, 0, 0, tiled=True
    )


def gathered_copies(value, axis, dim):
    return in_order(copy_for_each(value, axis), dim)


def block_filter(matrix, kept_blocks):
    count_rows, count_cols = kept_blocks.shape
    blocked = matrix.reshape(count_rows, BS, count_cols, BS)
    return jnp.where(kept_blocks[:, None, :, None], blocked, jnp.zeros_like(blocked)).reshape(
        matrix.shape
    )


def column_subset(matrix, layer_count, layer_id):
    reshaped = matrix.reshape(matrix.shape[0], -1, layer_count, BS)
    picked = lax.dynamic_index_in_dim(reshaped, layer_id, 2, keepdims=False)
    return picked.reshape(matrix.shape[0], -1)


def row_subset(matrix, layer_count, layer_id):
    reshaped = matrix.reshape(-1, layer_count, BS, matrix.shape[1])
    picked = lax.dynamic_index_in_dim(reshaped, layer_id, 1, keepdims=False)
    return picked.reshape(-1, matrix.shape[1])


def multiply(left_matrix, right_matrix, layer_count, layer_id):
    left_part = column_subset(left_matrix, layer_count, layer_id)
    right_part = row_subset(right_matrix, layer_count, layer_id)
    row_strip = lax.all_gather(right_part, "row", axis=0, tiled=True)
    return jnp.dot(
        gathered_copies(left_part, "col", 1), row_strip, preferred_element_type=jnp.float32
    )


def shards(density, pattern, holder, slot_index, atom_index, derivative):
    layer_count = lax.axis_size("layer")
    layer_id = lax.axis_index("layer")
    grid_row = lax.axis_index("row")
    grid_col = lax.axis_index("col")
    row_blocks, col_blocks = pattern.shape
    global_rows = grid_row * row_blocks + jnp.arange(row_blocks, dtype=jnp.int32)
    global_cols = grid_col * col_blocks + jnp.arange(col_blocks, dtype=jnp.int32)
    kept_blocks = (pattern == 1) | (global_rows[:, None] == global_cols[None, :])
    filtered = block_filter(density, kept_blocks)
    partial_square = multiply(filtered, filtered, layer_count, layer_id)
    share_blocks = row_blocks // layer_count
    square_share = lax.psum_scatter(
        partial_square, "layer", scatter_dimension=0, tiled=True
    ).astype(jnp.bfloat16)
    square = lax.all_gather(square_share, "layer", axis=0, tiled=True)
    partial_cube = multiply(square, filtered, layer_count, layer_id)
    cube_share = lax.psum_scatter(partial_cube, "layer", scatter_dimension=0, tiled=True)
    kept_share = lax.dynamic_slice_in_dim(kept_blocks, layer_id * share_blocks, share_blocks, 0)
    purified = block_filter(
        3.0 * square_share.astype(jnp.float32) - 2.0 * cube_share, kept_share
    ).astype(jnp.bfloat16)
    held_blocks = (
        purified.reshape(share_blocks, BS, col_blocks, BS)
        .transpose(0, 2, 1, 3)
        .reshape(share_blocks * col_blocks, BS, BS)
    )
    holders_total = lax.axis_size("row") * lax.axis_size("col")
    entry_count = slot_index.shape[0]
    capacity = max(2, 2 * entry_count // holders_total)
    targets = holder[:, 0]
    target_hot = (targets[:, None] == jnp.arange(holders_total, dtype=jnp.int32)[None, :]).astype(
        jnp.int32
    )
    rank_values = jnp.sum(target_hot * (jnp.cumsum(target_hot, axis=0) - 1), axis=1)
    positions = targets * capacity + rank_values
    position_hot = (
        positions[None, :] == jnp.arange(holders_total * capacity, dtype=jnp.int32)[:, None]
    )
    requests = jnp.sum(jnp.where(position_hot, slot_index[None, :], 0), axis=1).reshape(
        holders_total, capacity
    )
    fetched = jnp.take(
        held_blocks,
        lax.all_to_all(requests, ("row", "col"), split_axis=0, concat_axis=0, tiled=True),
        axis=0,
    )
    returned = lax.all_to_all(fetched, ("row", "col"), split_axis=0, concat_axis=0, tiled=True)
    arrived = jnp.take(returned.reshape(holders_total * capacity, BS, BS), positions, axis=0)
    contrib = jnp.einsum("eij,exij->xe", arrived, derivative, preferred_element_type=jnp.float32)
    atom_hot = (atom_index[:, None] == jnp.arange(ATOM_DEV, dtype=jnp.int32)[None, :]).astype(
        jnp.float32
    )
    return -2.0 * jnp.dot(contrib, atom_hot, precision=lax.Precision.HIGHEST)


def solution(mesh):
    return jax.shard_map(
        shards,
        mesh=mesh,
        in_specs=(
            P("row", "col"),
            P("row", "col"),
            P(("layer", "row", "col"), None),
            P(("layer", "row", "col")),
            P(("layer", "row", "col")),
            P(("layer", "row", "col"), None, None, None),
        ),
        out_specs=P(None, ("layer", "row", "col")),
        check_vma=False,
    )
```

profile of v0, /device:TPU:1, one launch (start us, length us, event | category | flops | bytes accessed | tf_op | source)
XLA Modules:
  0.0 458.0 jit_solution(10009303842181600829)
XLA Ops:
  6.5 0.0 copy-start
  6.5 0.0 all-gather.6.cloned.1.call-start
  6.5 0.9 compare_or_fusion
  7.5 0.1 broadcast_bitcast_fusion
  7.6 2.3 dynamic-slice_select_fusion
  9.9 0.0 all-gather.6.cloned.1.call-update
  9.9 0.0 reduce-scatter.3.cloned.1.call-start
  10.0 0.1 copy.39
  10.1 6.5 %copy.40 = bf16[512,4096]{0,1:T(8,128)(2,1)} copy(bf16[512,4096]{1,0:T(8,128)(2,1)} %param.6) | data formatting | bytes 8388608 | tf_op args[0]
  16.6 0.1 broadcast_in_dim.104
  16.7 1.3 dynamic-slice_select_fusion.1
  18.1 0.1 broadcast_in_dim.109
  18.2 7.4 %all_to_all.30 = bf16[2,512,1024]{1,2,0:T(8,128)(2,1)} all-to-all(bf16[2,512,1024]{1,2,0:T(8,128)(2,1)S(1)} %broadcast_in_dim.109), channel_id=1, replica_groups=mesh['layer'=4,'row'=16,'col'=2] {'col'}, dimensions={0} | all-to-all | bytes 4194304 | tf_op jit(solution)/shard_map/all_to_all | solution.py:18
  25.6 99.1 %all-gather.6.cloned.1.call-done = bf16[1,1,2048,4096]{3,2,1,0:T(8,128)(2,1)} async-done(((bf16[1,1,128,4096]{3,2,1,0:T(8,128)(2,1)}), bf16[1,1,2048,4096]{3,2,1,0:T(8,128)(2,1)}) %all-gather.6.cloned.1.call-update) | async-done | bytes 16777232 | tf_op jit(solution)/shard_map/all_gather | solution.py:50
  124.7 15.1 %fusion.2 = f32[512,4096]{1,0:T(8,128)} fusion(bf16[512,2048]{0,1:T(8,128)(2,1)} %bitcast.69, bf16[1,1,2048,4096]{3,2,1,0:T(8,128)(2,1)} %all-gather.6.cloned.1.call-done), kind=kOutput, calls=%fused_computation.4 | convolution fusion | flops 8589934592 | bytes 27262976 | tf_op jit(solution)/shard_map/dot_general | solution.py:51
  139.9 0.0 reduce-scatter.3.cloned.1.call-update
  139.9 0.0 all-gather.4.cloned.1.call-start
  139.9 80.2 %reduce-scatter.3.cloned.1.call-done = f32[128,4096]{1,0:T(8,128)} async-done(((f32[512,4096]{1,0:T(8,128)}), f32[128,4096]{1,0:T(8,128)}) %reduce-scatter.3.cloned.1.call-update) | async-done | bytes 2097168 | tf_op jit(solution)/shard_map/reduce_scatter | solution.py:68
  220.2 2.7 convert_element_type.14
  222.9 0.0 all-gather.4.cloned.1.call-update
  222.9 0.0 reduce-scatter.5.cloned.1.call-start
  222.9 48.0 %all-gather.4.cloned.1.call-done = bf16[512,4096]{1,0:T(8,128)(2,1)} async-done(((bf16[128,4096]{1,0:T(8,128)(2,1)}), bf16[512,4096]{1,0:T(8,128)(2,1)}) %all-gather.4.cloned.1.call-update) | async-done | bytes 4194320 | tf_op jit(solution)/shard_map/all_gather | solution.py:71
  271.0 7.8 %reshape.121 = bf16[512,8,4,128]{3,2,1,0:T(4,128)(2,1)} reshape(bf16[512,4096]{1,0:T(8,128)(2,1)} %all-gather.4.cloned.1.call-done) | data formatting | bytes 8388608 | tf_op jit(solution)/shard_map/reshape | solution.py:36
  278.7 5.7 %constant_dynamic-slice_fusion = bf16[512,8,1,128]{3,2,1,0:T(2,128)(2,1)} fusion(bf16[512,8,4,128]{3,2,1,0:T(4,128)(2,1)} %reshape.121, s32[]{:T(128)S(6)} %select_n.68), kind=kLoop, calls=%fused_computation.36 | loop fusion | bytes 2097156 | tf_op jit(solution)/shard_map/jit(dynamic_index_in_dim)/dynamic_slice | solution.py:37
  284.4 5.8 %copy.48 = bf16[512,8,1,128]{0,3,1,2:T(8,128)(2,1)} copy(bf16[512,8,1,128]{3,2,1,0:T(2,128)(2,1)} %constant_dynamic-slice_fusion) | data formatting | bytes 2097152
  290.3 1.4 broadcast_in_dim.115
  291.6 5.8 %all_to_all.31 = bf16[2,512,1024]{1,2,0:T(8,128)(2,1)S(1)} all-to-all(bf16[2,512,1024]{1,2,0:T(8,128)(2,1)S(1)} %broadcast_in_dim.115), channel_id=1, replica_groups=mesh['layer'=4,'row'=16,'col'=2] {'col'}, dimensions={0} | all-to-all | bytes 4194304 | tf_op jit(solution)/shard_map/all_to_all | solution.py:18
  297.4 14.5 %fusion = f32[512,4096]{1,0:T(8,128)} fusion(bf16[512,2048]{0,1:T(8,128)(2,1)S(1)} %bitcast.70, bf16[1,1,2048,4096]{3,2,1,0:T(8,128)(2,1)} %all-gather.6.cloned.1.call-done), kind=kOutput, calls=%fused_computation.2 | convolution fusion | flops 8589934592 | bytes 27262976 | tf_op jit(solution)/shard_map/dot_general | solution.py:51
  311.9 0.0 copy-start.1
  311.9 0.0 copy-start.2
  311.9 0.0 reduce-scatter.5.cloned.1.call-update
  312.0 0.6 copy-done.1
  312.6 0.1 fusion.8
  312.7 0.1 reduce_window_sum.11
  312.7 0.2 select_reduce_fusion.1
  312.9 0.0 copy-done.2
  312.9 0.1 select_reduce_fusion
  313.0 0.7 all_to_all.19
  313.7 7.3 %all-to-all-start = ((s32[32,1,2]{2,1,0:T(1,128)}), s32[32,1,2]{2,1,0:T(1,128)S(1)}, u32[]{:S(2)}, u32[]{:S(2)}) async-start(s32[32,1,2]{2,1,0:T(1,128)} %bitcast.3), calls=%async_computation | async-start | bytes 32768 | tf_op jit(solution)/shard_map/all_to_all | solution.py:100
  321.1 0.1 broadcast_bitcast_fusion.1
  321.2 6.8 %all-to-all-done = s32[32,1,2]{2,1,0:T(1,128)S(1)} async-done(((s32[32,1,2]{2,1,0:T(1,128)}), s32[32,1,2]{2,1,0:T(1,128)S(1)}, u32[]{:S(2)}, u32[]{:S(2)}) %all-to-all-start) | async-done | bytes 288 | tf_op jit(solution)/shard_map/all_to_all | solution.py:100
  328.0 0.1 copy.37
  328.1 0.1 copy.44
  328.2 0.1 reshape.128
  328.3 0.1 copy.38
  328.4 64.2 %reduce-scatter.5.cloned.1.call-done = f32[128,4096]{1,0:T(8,128)} async-done(((f32[512,4096]{1,0:T(8,128)}), f32[128,4096]{1,0:T(8,128)}) %reduce-scatter.5.cloned.1.call-update) | async-done | bytes 2097168 | tf_op jit(solution)/shard_map/reduce_scatter | solution.py:73
  392.7 2.6 fusion.7
  395.3 0.2 copy.50
  395.5 1.4 copy.57
  397.0 3.4 gather_fusion
  400.4 3.2 broadcast_select_fusion
  403.5 7.7 %all-to-all-start.3 = ((bf16[32,2,128,128]{3,2,1,0:T(8,128)(2,1)}), bf16[32,2,128,128]{3,2,1,0:T(8,128)(2,1)}, u32[]{:S(2)}, u32[]{:S(2)}) async-start(bf16[32,2,128,128]{3,2,1,0:T(8,128)(2,1)} %broadcast_select_fusion), calls=%async_computation.5 | async-start | bytes 4194304 | tf_op jit(solution)/shard_map/all_to_all | solution.py:103
  411.3 27.9 %all-to-all-done.3 = bf16[32,2,128,128]{3,2,1,0:T(8,128)(2,1)} async-done(((bf16[32,2,128,128]{3,2,1,0:T(8,128)(2,1)}), bf16[32,2,128,128]{3,2,1,0:T(8,128)(2,1)}, u32[]{:S(2)}, u32[]{:S(2)}) %all-to-all-start.3) | async-done | bytes 2097184 | tf_op jit(solution)/shard_map/all_to_all | solution.py:103
  439.1 3.3 gather_fusion.1
  442.4 1.4 select_bitcast_fusion
  443.8 0.0 copy-done
  443.8 0.0 copy-start.3
  443.8 6.9 %fusion.4 = f32[32,1,3,1]{2,1,3,0:T(1,128)S(1)} fusion(bf16[32,3,128,128]{3,2,1,0:T(8,128)(2,1)S(1)} %copy-done, bf16[32,128,128,1]{2,1,0,3:T(8,128)(2,1)S(1)} %select_bitcast_fusion), kind=kOutput, calls=%fused_computation.6 | convolution fusion | flops 3145728 | bytes 4194688 | tf_op jit(solution)/shard_map/eij,exij->xe/dot_general | solution.py:105
  450.7 0.0 copy-done.3
  450.7 0.8 convolution_multiply_fusion
  (13 shorter events, 0.2 us)
Async XLA Ops:
  6.5 437.2 %copy-start = (bf16[32,3,128,128]{3,2,1,0:T(8,128)(2,1)S(1)}, bf16[32,3,128,128]{3,2,1,0:T(8,128)(2,1)}, u32[]{:S(2)}) copy-start(bf16[32,3,128,128]{3,2,1,0:T(8,128)(2,1)} %param.11) | copy-start | bytes 9437188
  6.5 118.2 %all-gather.6.cloned.1.call-start = ((), (), s32[]{:S(2)}) async-start(), calls=%async_computation.9 | async-start | bytes 17825792 | tf_op jit(solution)/shard_map/all_gather | solution.py:50
  9.9 210.2 %reduce-scatter.3.cloned.1.call-start = ((), (), s32[]{:S(2)}) async-start(), calls=%async_computation.6 | async-start | bytes 10485760 | tf_op jit(solution)/shard_map/reduce_scatter | solution.py:68
  139.9 131.1 %all-gather.4.cloned.1.call-start = ((), (), s32[]{:S(2)}) async-start(), calls=%async_computation.7 | async-start | bytes 5242880 | tf_op jit(solution)/shard_map/all_gather | solution.py:71
  222.9 169.8 %reduce-scatter.5.cloned.1.call-start = ((), (), s32[]{:S(2)}) async-start(), calls=%async_computation.8 | async-start | bytes 10485760 | tf_op jit(solution)/shard_map/reduce_scatter | solution.py:73
  311.9 0.7 copy-start.1
  311.9 1.0 copy-start.2
  313.7 14.3 %all-to-all-start = ((s32[32,1,2]{2,1,0:T(1,128)}), s32[32,1,2]{2,1,0:T(1,128)S(1)}, u32[]{:S(2)}, u32[]{:S(2)}) async-start(s32[32,1,2]{2,1,0:T(1,128)} %bitcast.3), calls=%async_computation | async-start | bytes 32768 | tf_op jit(solution)/shard_map/all_to_all | solution.py:100
  403.5 35.6 %all-to-all-start.3 = ((bf16[32,2,128,128]{3,2,1,0:T(8,128)(2,1)}), bf16[32,2,128,128]{3,2,1,0:T(8,128)(2,1)}, u32[]{:S(2)}, u32[]{:S(2)}) async-start(bf16[32,2,128,128]{3,2,1,0:T(8,128)(2,1)} %broadcast_select_fusion), calls=%async_computation.5 | async-start | bytes 4194304 | tf_op jit(solution)/shard_map/all_to_all | solution.py:103
  443.8 6.9 %copy-start.3 = (s32[32]{0:T(128)S(1)}, s32[32]{0:T(128)}, u32[]{:S(2)}) copy-start(s32[32]{0:T(128)} %param.10) | copy-start | bytes 388
Sparse Core Ops, SparseCore 0:
  10.0 114.6 all-gather.5
  140.0 80.1 reduce-scatter.2
  223.0 47.9 all-gather.3
  312.1 80.5 reduce-scatter.4
where the time goes:
time: 460 us; the launch traced here: 458 us
  waiting for transfers between devices  326 us (71%)
  local copies, waits for them, and re-layouts  37.8 us (8%)
  matrix products  37.4 us (8%)
  starting transfers between devices  15.2 us (3%)
  other arithmetic  14.8 us (3%)
  between operations  13.3 us (3%)
  blocking collectives  13.2 us (3%)
    all_gather x1, waiting for transfers between devices, multiply(): row_strip = lax.all_gather(right_part, 'row', axis=0, tiled=True)  99.1 us
    reduce_scatter x1, waiting for transfers between devices, shards(): lax.psum_scatter(partial_square, 'layer', scatter_dimension=0, tiled=True)  80.2 us
    reduce_scatter x1, waiting for transfers between devices, shards(): lax.psum_scatter(partial_cube, 'layer', scatter_dimension=0, tiled=True)  64.2 us
    all_gather x1, waiting for transfers between devices, shards(): square = lax.all_gather(square_share, 'layer', axis=0, tiled=True)  48 us
    dot_general x2, matrix products, multiply(): jnp.dot(gathered_copies(left_part, 'col', 1), row_strip, preferred_elemen...  29.7 us
    all_to_all x1, waiting for transfers between devices, shards(): lax.all_to_all(fetched, ('row', 'col'), split_axis=0, concat_axis=0, tile...  27.9 us
    unnamed x13, local copies, waits for them, and re-layouts  13.3 us
    all_to_all x2, blocking collectives, copy_for_each(): lax.all_to_all(jnp.broadcast_to(value[None], (length, *value.shape)), axi...  13.2 us
  transfers between devices with their start and end apart: 6, of which 6 were waited for; matrix products, arithmetic and copies ran while one was open for 2% of the time, Pallas kernels for 0%

commit v1 on v0

v1 whole, which is shorter than its diff:
```python
import jax
import jax.numpy as jnp
from jax import lax
from jax.sharding import Mesh, PartitionSpec as P

BS = 128
ATOM_DEV = 8


def kept_of(pattern, grid_row, grid_col):
    row_blocks, col_blocks = pattern.shape
    global_rows = grid_row * row_blocks + jnp.arange(row_blocks, dtype=jnp.int32)
    global_cols = grid_col * col_blocks + jnp.arange(col_blocks, dtype=jnp.int32)
    return (pattern == 1) | (global_rows[:, None] == global_cols[None, :])


def block_filter(matrix, kept_blocks):
    count_rows, count_cols = kept_blocks.shape
    blocked = matrix.reshape(count_rows, BS, count_cols, BS)
    return jnp.where(kept_blocks[:, None, :, None], blocked, jnp.zeros_like(blocked)).reshape(
        matrix.shape
    )


def purify(filtered, kept_blocks):
    x = lax.axis_index("layer")
    bf = jnp.bfloat16
    right = lax.dynamic_slice_in_dim(filtered, x * 1024, 1024, 1)
    right = lax.all_gather(right, "z", axis=0, tiled=True)
    rows = lax.dynamic_slice_in_dim(filtered, x * BS, BS, 0)
    piece = rows.reshape(BS, 2, 4, 512).transpose(2, 0, 1, 3).reshape(4, BS, 1024)
    piece = lax.all_to_all(piece, "y", 0, 0, tiled=True)
    left = lax.all_gather(piece, "layer", axis=0, tiled=False)
    left = lax.all_gather(left, "col", axis=0, tiled=False)
    left = left.transpose(2, 1, 3, 0, 4).reshape(2048, 2048)

    def product(factor):
        partial = jnp.dot(left, factor, preferred_element_type=jnp.float32).astype(bf)
        return lax.psum_scatter(partial, "y", scatter_dimension=0, tiled=True)

    square = product(right)
    cube = product(lax.all_gather(square, "z", axis=0, tiled=True))
    kept = lax.dynamic_slice_in_dim(kept_blocks, x * 8, 8, 1)
    purified = block_filter(
        3.0 * square.astype(jnp.float32) - 2.0 * cube.astype(jnp.float32), kept
    ).astype(bf)
    blocks = purified.reshape(4, BS, 8, BS).transpose(0, 2, 1, 3)
    return lax.all_to_all(blocks, "layer", 0, 0, tiled=True).reshape(32, BS, BS)


def select(indices, blocks):
    hot = indices[:, None] == jnp.arange(blocks.shape[0], dtype=jnp.int32)[None, :]
    flat = jnp.dot(hot.astype(blocks.dtype), blocks.reshape(blocks.shape[0], BS * BS))
    return flat.reshape(-1, BS, BS)


def shards(density, pattern, holder, slot_index, atom_index, derivative):
    grid_row = lax.axis_index("z") * 4 + lax.axis_index("y")
    kept_blocks = kept_of(pattern, grid_row, lax.axis_index("col"))
    held_blocks = purify(block_filter(density, kept_blocks), kept_blocks)
    holders_total = 32
    capacity = 2
    targets = holder[:, 0]
    entries = jnp.arange(targets.shape[0], dtype=jnp.int32)
    earlier = (targets[:, None] == targets[None, :]) & (entries[None, :] < entries[:, None])
    rank_values = jnp.sum(earlier.astype(jnp.int32), axis=1)
    positions = targets * capacity + rank_values
    position_hot = (
        positions[None, :] == jnp.arange(holders_total * capacity, dtype=jnp.int32)[:, None]
    )
    requests = jnp.sum(jnp.where(position_hot, slot_index[None, :], 0), axis=1).reshape(
        holders_total, capacity
    )
    axes = ("z", "y", "col")
    asked = lax.all_to_all(requests, axes, split_axis=0, concat_axis=0, tiled=True).reshape(-1)
    fetched = select(asked, held_blocks).reshape(holders_total, capacity, BS, BS)
    returned = lax.all_to_all(fetched, axes, split_axis=0, concat_axis=0, tiled=True)
    arrived = select(positions, returned.reshape(holders_total * capacity, BS, BS))
    contrib = jnp.einsum("eij,exij->xe", arrived, derivative, preferred_element_type=jnp.float32)
    atom_hot = (atom_index[:, None] == jnp.arange(ATOM_DEV, dtype=jnp.int32)[None, :]).astype(
        jnp.float32
    )
    return -2.0 * jnp.dot(contrib, atom_hot, precision=lax.Precision.HIGHEST)


def solution(mesh):
    split = Mesh(mesh.devices.reshape(4, 4, 4, 2), ("layer", "z", "y", "col"))
    every = ("layer", "z", "y", "col")
    return jax.shard_map(
        shards,
        mesh=split,
        in_specs=(
            P(("z", "y"), "col"),
            P(("z", "y"), "col"),
            P(every, None),
            P(every),
            P(every),
            P(every, None, None, None),
        ),
        out_specs=P(None, every),
        check_vma=False,
    )
```

time: 460 us -> 422 us (0.917)
  waiting for transfers between devices: 326 us -> 276 us
  local copies, waits for them, and re-layouts: 37.8 us -> 46.2 us
  other arithmetic: 14.8 us -> 6.7 us
  blocking collectives: 13.2 us -> 19.1 us
    reduce_scatter x2, waiting for transfers between devices: 144 us -> 86.5 us  [product(): return lax.psum_scatter(partial, 'y', scatter_dimension=0, tiled=True)]
    transpose x0 -> x3, local copies, waits for them, and re-layouts: none -> 17.6 us  [the longest x1 16.5 us: purify(): left = left.transpose(2, 1, 3, 0, 4).reshape(2048, 2048)]
    reshape x2 -> x0, local copies, waits for them, and re-layouts: 9.17 us -> none  [the longest x1 7.75 us: column_subset(): reshaped = matrix.reshape(matrix.shape[0], -1, layer_count, BS)]
    all_to_all x2 -> x3, waiting for transfers between devices: 34.7 us -> 42.6 us  [the longest x1 27.9 us: shards(): lax.all_to_all(fetched, axes, split_axis=0, concat_axis=0, tiled=True)]
    gather x2 -> x0, local copies, waits for them, and re-layouts: 6.66 us -> none  [the longest x1 3.39 us: shards(): jnp.take(held_blocks, lax.all_to_all(requests, ('row', 'col'), split_axis...]
    unnamed x13, local copies, waits for them, and re-layouts: 13.3 us -> 19.5 us
    all_to_all x2 -> x1, blocking collectives: 13.2 us -> 19.1 us  [purify(): piece = lax.all_to_all(piece, 'y', 0, 0, tiled=True)]
    dot_general x2 -> x4, matrix products: 29.7 us -> 32.7 us  [the longest x2 27.6 us: product(): jnp.dot(left, factor, preferred_element_type=jnp.float32).astype(bf)]
  transfers between devices with their start and end apart: 6 -> 9, of which waited for: 6 -> 8; matrix products, arithmetic and copies ran while one was open for 2% -> 8% of each run, Pallas kernels for 0% -> 0%
where the time goes in v1:
time: 422 us; the launch traced here: 421 us
  waiting for transfers between devices  276 us (65%)
  local copies, waits for them, and re-layouts  46.2 us (11%)
  matrix products  41.5 us (10%)
  blocking collectives  19.1 us (5%)
  starting transfers between devices  18 us (4%)
  between operations  13.6 us (3%)
  other arithmetic  6.7 us (2%)
    reduce_scatter x2, waiting for transfers between devices, product(): return lax.psum_scatter(partial, 'y', scatter_dimension=0, tiled=True)  86.5 us
    all_gather x1, waiting for transfers between devices, purify(): left = lax.all_gather(piece, 'layer', axis=0, tiled=False)  49.9 us
    all_gather x1, waiting for transfers between devices, purify(): cube = product(lax.all_gather(square, 'z', axis=0, tiled=True))  49.7 us
    all_to_all x1, waiting for transfers between devices, shards(): lax.all_to_all(fetched, axes, split_axis=0, concat_axis=0, tiled=True)  27.9 us
    dot_general x2, matrix products, product(): jnp.dot(left, factor, preferred_element_type=jnp.float32).astype(bf)  27.6 us
    all_gather x1, waiting for transfers between devices, purify(): right = lax.all_gather(right, 'z', axis=0, tiled=True)  24.5 us
    all_gather x1, waiting for transfers between devices, purify(): left = lax.all_gather(left, 'col', axis=0, tiled=False)  22.4 us
    unnamed x13, local copies, waits for them, and re-layouts  19.5 us
  transfers between devices with their start and end apart: 9, of which 8 were waited for; matrix products, arithmetic and copies ran while one was open for 8% of the time, Pallas kernels for 0%

profile of v1, /device:TPU:1, one launch (start us, length us, event | category | flops | bytes accessed | tf_op | source)
XLA Modules:
  0.0 420.7 jit_solution(4899943230154906097)
XLA Ops:
  6.5 0.0 copy-start
  6.5 0.0 all-gather.11.cloned.1.call-start
  6.5 0.9 compare_or_fusion
  7.5 0.1 copy.40
  7.6 6.5 %copy.41 = bf16[512,4096]{0,1:T(8,128)(2,1)} copy(bf16[512,4096]{1,0:T(8,128)(2,1)} %param.6) | data formatting | bytes 8388608 | tf_op args[0]
  14.0 1.1 broadcast_in_dim.56
  15.2 3.3 bitcast_select_fusion
  18.4 0.0 copy-start.1
  18.5 2.0 copy-done.1
  20.4 0.1 constant_dynamic-slice_fusion
  20.6 0.1 copy.42
  20.6 19.1 %all_to_all.24 = bf16[4,128,1024]{1,2,0:T(8,128)(2,1)} all-to-all(bf16[4,128,1024]{1,2,0:T(8,128)(2,1)S(1)} %bitcast.96), channel_id=1, replica_groups=mesh['layer'=4,'z'=4,'y'=4,'col'=2] {'y'}, dimensions={0} | all-to-all | bytes 2097152 | tf_op jit(solution)/shard_map/all_to_all | solution.py:32
  39.7 2.3 copy.43
  42.0 0.0 all-gather.11.cloned.1.call-update
  42.0 0.0 all-gather.13.cloned.1.call-start
  42.1 49.9 %all-gather.11.cloned.1.call-done = bf16[16,128,1024]{2,1,0:T(8,128)(2,1)} async-done(((bf16[4,128,1024]{2,1,0:T(8,128)(2,1)}), bf16[16,128,1024]{2,1,0:T(8,128)(2,1)}) %all-gather.11.cloned.1.call-update) | async-done | bytes 4194320 | tf_op jit(solution)/shard_map/all_gather | solution.py:33
  92.0 0.0 all-gather.13.cloned.1.call-update
  92.0 0.0 all-gather.7.cloned.1.call-start
  92.0 2.3 constant_dynamic-slice_fusion.2
  94.3 0.0 all-gather.7.cloned.1.call-update
  94.3 0.2 reduce-scatter.3.cloned.1.call-start
  94.6 22.4 %all-gather.13.cloned.1.call-done = bf16[8,4,128,1024]{3,2,1,0:T(8,128)(2,1)} async-done(((bf16[4,4,128,1024]{3,2,1,0:T(8,128)(2,1)}), bf16[8,4,128,1024]{3,2,1,0:T(8,128)(2,1)}) %all-gather.13.cloned.1.call-update) | async-done | bytes 8388624 | tf_op jit(solution)/shard_map/all_gather | solution.py:34
  117.0 16.5 %copy.44 = bf16[4,4,128,2,1024]{4,3,2,1,0:T(2,128)(2,1)} copy(bf16[4,4,128,2,1024]{4,2,0,1,3:T(8,128)(2,1)} %bitcast.93) | data formatting | bytes 16777216 | tf_op jit(solution)/shard_map/transpose | solution.py:35
  133.5 10.1 %copy.56 = bf16[256,8,2,1024]{3,1,2,0:T(8,128)(2,1)} copy(bf16[256,8,2,1024]{3,2,1,0:T(2,128)(2,1)} %bitcast.89) | data formatting | bytes 16777216
  143.6 24.5 %all-gather.7.cloned.1.call-done = bf16[2048,1024]{0,1:T(8,128)(2,1)} async-done(((bf16[512,1024]{0,1:T(8,128)(2,1)}), bf16[2048,1024]{0,1:T(8,128)(2,1)}) %all-gather.7.cloned.1.call-update) | async-done | bytes 4194320 | tf_op jit(solution)/shard_map/all_gather | solution.py:29
  168.1 13.9 %convolution_convert_fusion.1 = bf16[2048,1024]{1,0:T(8,128)(2,1)} fusion(bf16[2048,2048]{1,0:T(8,128)(2,1)} %bitcast.91, bf16[2048,1024]{0,1:T(8,128)(2,1)} %all-gather.7.cloned.1.call-done), kind=kOutput, calls=%fused_computation.4 | convolution fusion | flops 8592031744 | bytes 16777216 | tf_op jit(solution)/shard_map/dot_general | solution.py:38
  181.9 0.0 reduce-scatter.3.cloned.1.call-update
  181.9 0.0 all-gather.9.cloned.1.call-start
  182.0 47.2 %reduce-scatter.3.cloned.1.call-done = bf16[512,1024]{1,0:T(8,128)(2,1)} async-done(((bf16[2048,1024]{1,0:T(8,128)(2,1)}), bf16[512,1024]{1,0:T(8,128)(2,1)}) %reduce-scatter.3.cloned.1.call-update) | async-done | bytes 1048592 | tf_op jit(solution)/shard_map/reduce_scatter | solution.py:39
  229.2 0.0 all-gather.9.cloned.1.call-update
  229.2 0.0 reduce-scatter.5.cloned.1.call-start
  229.3 49.7 %all-gather.9.cloned.1.call-done = bf16[2048,1024]{1,0:T(8,128)(2,1)} async-done(((bf16[512,1024]{1,0:T(8,128)(2,1)}), bf16[2048,1024]{1,0:T(8,128)(2,1)}) %all-gather.9.cloned.1.call-update) | async-done | bytes 4194320 | tf_op jit(solution)/shard_map/all_gather | solution.py:42
  279.0 13.8 %convolution_convert_fusion = bf16[2048,1024]{1,0:T(8,128)(2,1)} fusion(bf16[2048,2048]{1,0:T(8,128)(2,1)} %bitcast.92, bf16[2048,1024]{1,0:T(8,128)(2,1)} %all-gather.9.cloned.1.call-done), kind=kOutput, calls=%fused_computation.3 | convolution fusion | flops 8592031744 | bytes 16777216 | tf_op jit(solution)/shard_map/dot_general | solution.py:38
  292.8 0.0 copy-start.3
  292.8 0.0 copy-start.2
  292.8 0.0 reduce-scatter.5.cloned.1.call-update
  292.8 0.6 copy-done.3
  293.4 0.2 convert_reduce_fusion
  293.6 0.0 copy-done.2
  293.6 0.1 select_reduce_fusion
  293.7 0.7 all_to_all.15
  294.4 6.6 %all-to-all-start = ((s32[32,1,2]{2,1,0:T(1,128)}), s32[32,1,2]{2,1,0:T(1,128)S(1)}, u32[]{:S(2)}, u32[]{:S(2)}) async-start(s32[32,1,2]{2,1,0:T(1,128)} %bitcast.4), calls=%async_computation | async-start | bytes 32768 | tf_op jit(solution)/shard_map/all_to_all | solution.py:75
  301.1 0.1 constant_dynamic-slice_fusion.1
  301.1 39.2 %reduce-scatter.5.cloned.1.call-done = bf16[512,1024]{1,0:T(8,128)(2,1)} async-done(((bf16[2048,1024]{1,0:T(8,128)(2,1)}), bf16[512,1024]{1,0:T(8,128)(2,1)}) %reduce-scatter.5.cloned.1.call-update) | async-done | bytes 1048592 | tf_op jit(solution)/shard_map/reduce_scatter | solution.py:39
  340.4 0.2 broadcast_in_dim.54
  340.6 2.2 fusion.9
  342.8 0.3 copy.57
  343.1 1.1 bitcast_bitcast_fusion.1
  344.2 0.0 all-to-all-done
  344.2 4.3 %all-to-all-start.2 = ((bf16[4,8,128,128]{3,1,2,0:T(8,128)(2,1)}), bf16[4,8,128,128]{3,1,2,0:T(8,128)(2,1)}, u32[]{:S(2)}, u32[]{:S(2)}) async-start(bf16[4,8,128,128]{3,1,2,0:T(8,128)(2,1)} %bitcast_bitcast_fusion.1), calls=%async_computation.4 | async-start | bytes 2097152 | tf_op jit(solution)/shard_map/all_to_all | solution.py:48
  348.4 0.1 copy.39
  348.5 14.7 %all-to-all-done.2 = bf16[4,8,128,128]{3,1,2,0:T(8,128)(2,1)} async-done(((bf16[4,8,128,128]{3,1,2,0:T(8,128)(2,1)}), bf16[4,8,128,128]{3,1,2,0:T(8,128)(2,1)}, u32[]{:S(2)}, u32[]{:S(2)}) %all-to-all-start.2) | async-done | bytes 1048608 | tf_op jit(solution)/shard_map/all_to_all | solution.py:48
  363.2 2.0 fusion.10
  365.1 2.1 copy.46
  367.3 6.8 %all-to-all-start.3 = ((bf16[32,2,128,128]{3,2,1,0:T(8,128)(2,1)}), bf16[32,2,128,128]{3,2,1,0:T(8,128)(2,1)}, u32[]{:S(2)}, u32[]{:S(2)}) async-start(bf16[32,2,128,128]{3,2,1,0:T(8,128)(2,1)} %copy.46), calls=%async_computation.5 | async-start | bytes 4194304 | tf_op jit(solution)/shard_map/all_to_all | solution.py:77
  374.1 27.9 %all-to-all-done.3 = bf16[32,2,128,128]{3,2,1,0:T(8,128)(2,1)} async-done(((bf16[32,2,128,128]{3,2,1,0:T(8,128)(2,1)}), bf16[32,2,128,128]{3,2,1,0:T(8,128)(2,1)}, u32[]{:S(2)}, u32[]{:S(2)}) %all-to-all-start.3) | async-done | bytes 2097184 | tf_op jit(solution)/shard_map/all_to_all | solution.py:77
  401.9 3.1 fusion.6
  405.0 0.0 copy-done
  405.0 0.0 copy-start.4
  405.1 8.0 %fusion = f32[32,1,3,1]{2,1,3,0:T(1,128)S(1)} fusion(bf16[32,3,128,128]{3,2,1,0:T(8,128)(2,1)S(1)} %copy-done, bf16[32,128,128,1]{2,0,1,3:T(8,128)(2,1)S(1)} %fusion.6), kind=kOutput, calls=%fused_computation.1 | convolution fusion | flops 3145728 | bytes 4194688 | tf_op jit(solution)/shard_map/eij,exij->xe/dot_general | solution.py:79
  413.1 0.0 copy-done.4
  413.1 0.8 convolution_multiply_fusion
  (4 shorter events, 0.0 us)
Async XLA Ops:
  6.5 398.5 %copy-start = (bf16[32,3,128,128]{3,2,1,0:T(8,128)(2,1)S(1)}, bf16[32,3,128,128]{3,2,1,0:T(8,128)(2,1)}, u32[]{:S(2)}) copy-start(bf16[32,3,128,128]{3,2,1,0:T(8,128)(2,1)} %param.11) | copy-start | bytes 9437188
  6.5 85.4 %all-gather.11.cloned.1.call-start = ((), (), s32[]{:S(2)}) async-start(), calls=%async_computation.10 | async-start | bytes 5242880 | tf_op jit(solution)/shard_map/all_gather | solution.py:33
  18.4 2.0 copy-start.1
  42.0 75.0 %all-gather.13.cloned.1.call-start = ((), (), s32[]{:S(2)}) async-start(), calls=%async_computation.11 | async-start | bytes 12582912 | tf_op jit(solution)/shard_map/all_gather | solution.py:34
  92.0 76.1 %all-gather.7.cloned.1.call-start = ((), (), s32[]{:S(2)}) async-start(), calls=%async_computation.6 | async-start | bytes 5242880 | tf_op jit(solution)/shard_map/all_gather | solution.py:29
  94.3 134.9 %reduce-scatter.3.cloned.1.call-start = ((), (), s32[]{:S(2)}) async-start(), calls=%async_computation.7 | async-start | bytes 5242880 | tf_op jit(solution)/shard_map/reduce_scatter | solution.py:39
  181.9 97.0 %all-gather.9.cloned.1.call-start = ((), (), s32[]{:S(2)}) async-start(), calls=%async_computation.8 | async-start | bytes 5242880 | tf_op jit(solution)/shard_map/all_gather | solution.py:42
  229.2 111.1 %reduce-scatter.5.cloned.1.call-start = ((), (), s32[]{:S(2)}) async-start(), calls=%async_computation.9 | async-start | bytes 5242880 | tf_op jit(solution)/shard_map/reduce_scatter | solution.py:39
  292.8 0.7 copy-start.3
  292.8 0.8 copy-start.2
  294.4 49.7 %all-to-all-start = ((s32[32,1,2]{2,1,0:T(1,128)}), s32[32,1,2]{2,1,0:T(1,128)S(1)}, u32[]{:S(2)}, u32[]{:S(2)}) async-start(s32[32,1,2]{2,1,0:T(1,128)} %bitcast.4), calls=%async_computation | async-start | bytes 32768 | tf_op jit(solution)/shard_map/all_to_all | solution.py:75
  344.2 19.0 %all-to-all-start.2 = ((bf16[4,8,128,128]{3,1,2,0:T(8,128)(2,1)}), bf16[4,8,128,128]{3,1,2,0:T(8,128)(2,1)}, u32[]{:S(2)}, u32[]{:S(2)}) async-start(bf16[4,8,128,128]{3,1,2,0:T(8,128)(2,1)} %bitcast_bitcast_fusion.1), calls=%async_computation.4 | async-start | bytes 2097152 | tf_op jit(solution)/shard_map/all_to_all | solution.py:48
  367.3 34.7 %all-to-all-start.3 = ((bf16[32,2,128,128]{3,2,1,0:T(8,128)(2,1)}), bf16[32,2,128,128]{3,2,1,0:T(8,128)(2,1)}, u32[]{:S(2)}, u32[]{:S(2)}) async-start(bf16[32,2,128,128]{3,2,1,0:T(8,128)(2,1)} %copy.46), calls=%async_computation.5 | async-start | bytes 4194304 | tf_op jit(solution)/shard_map/all_to_all | solution.py:77
  405.0 8.0 %copy-start.4 = (s32[32]{0:T(128)S(1)}, s32[32]{0:T(128)}, u32[]{:S(2)}) copy-start(s32[32]{0:T(128)} %param.10) | copy-start | bytes 388
Sparse Core Ops, SparseCore 0:
  42.2 49.7 all-gather.10
  93.6 23.3 all-gather.12
  118.7 49.3 all-gather.6
  182.1 47.1 reduce-scatter.2
  230.8 48.1 all-gather.8
  292.9 47.4 reduce-scatter.4

commit v2 on v1

v2 whole, which is shorter than its diff:
```python
import jax
import jax.numpy as jnp
from jax import lax
from jax.experimental import pallas as pl
from jax.experimental.pallas import tpu as pltpu
from jax.sharding import Mesh, PartitionSpec as P

BS = 128
ATOM_DEV = 8
CHUNKS = 4
WIDE = 256
F32 = jnp.float32
BF16 = jnp.bfloat16
MESH = pl.DeviceIdType.MESH
COPIES = 130


class Links:
    def __init__(self, place, send_sems, recv_sems):
        self.place, self.send_sems, self.recv_sems = place, send_sems, recv_sems
        self.started = []
        self.count = 0

    def copy(self, src, dst, axis, step):
        number, self.count = self.count, self.count + 1
        length = 2 if axis == "col" else 4
        made = pltpu.make_async_remote_copy(
            src_ref=src,
            dst_ref=dst,
            send_sem=self.send_sems.at[number],
            recv_sem=self.recv_sems.at[number],
            device_id={axis: lax.rem(self.place[axis] + step + length, length)},
            device_id_type=MESH,
        )
        made.start()
        self.started.append(made)
        return made


class Ring:
    def __init__(self, links, axis, slot):
        self.links, self.axis, self.slot = links, axis, slot
        self.own = links.place[axis]

    def start(self):
        mine = self.slot(self.own)
        self.up = self.links.copy(mine, mine, self.axis, 1)
        self.down = self.links.copy(mine, mine, self.axis, -1)

    def forward(self):
        half = self.slot(self.own).shape[0] // 2
        self.up.wait_recv()
        lower = self.slot(lax.rem(self.own + 3, 4)).at[pl.ds(0, half)]
        self.up_half = self.links.copy(lower, lower, self.axis, 1)
        self.down.wait_recv()
        upper = self.slot(lax.rem(self.own + 1, 4)).at[pl.ds(half, half)]
        self.down_half = self.links.copy(upper, upper, self.axis, -1)

    def finish(self):
        self.up_half.wait_recv()
        self.down_half.wait_recv()


def purify_kernel(
    pattern, density, held_out,
    rows_in, cols_in, left, left_send, left_pass, right, square, part, sums_send, sums_recv, pure, held,
    in_sems, send_sems, recv_sems,
):
    x, z, y, c = (lax.axis_index(a) for a in ("layer", "z", "y", "col"))
    place = {"layer": x, "z": z, "y": y, "col": c}
    links = Links(place, send_sems, recv_sems)
    load_rows = pltpu.make_async_copy(
        density.at[pl.ds(pl.multiple_of(x * BS, BS), BS), :], rows_in, in_sems.at[0]
    )
    load_cols = pltpu.make_async_copy(
        density.at[:, pl.ds(pl.multiple_of(x * 1024, 1024), 1024)], cols_in, in_sems.at[1]
    )
    load_rows.start()
    load_cols.start()
    barrier = pltpu.get_barrier_semaphore()
    greeted = 0
    for axis, steps in (("y", (1, 3)), ("z", (1, 3)), ("layer", (1, 2, 3)), ("col", (1,))):
        length = 2 if axis == "col" else 4
        for step in steps:
            pl.semaphore_signal(
                barrier, inc=1, device_id={axis: lax.rem(place[axis] + step, length)},
                device_id_type=MESH,
            )
            greeted += 1

    def kept(row_block, col_block):
        inside = pattern[row_block, col_block] == 1
        return inside | ((z * 4 + y) * 4 + row_block == c * 32 + col_block)

    load_rows.wait()
    for b in range(32):
        block = rows_in[:, b * BS : (b + 1) * BS]
        block = jnp.where(kept(x, b), block, jnp.zeros_like(block))
        lane = (b // 16) * 512 + (b % 4) * BS
        left_send[(b % 16) // 4, :, lane : lane + BS] = block
    left[c, y, x] = left_send[y]
    pl.semaphore_wait(barrier, greeted)

    def over(step):
        return lax.rem(y + step, 4)

    y_up = links.copy(left_send.at[over(1)], left.at[c, y, x], "y", 1)
    y_down = links.copy(left_send.at[over(3)], left.at[c, y, x], "y", -1)
    far = left_send.at[over(2)]
    y_up_pass = links.copy(far.at[pl.ds(0, 64)], left_pass.at[0], "y", 1)
    y_down_pass = links.copy(far.at[pl.ds(64, 64)], left_pass.at[1], "y", -1)

    load_cols.wait()
    for b in range(8):
        for r in range(4):
            block = cols_in[r * BS : (r + 1) * BS, b * BS : (b + 1) * BS]
            block = jnp.where(kept(r, x * 8 + b), block, jnp.zeros_like(block))
            lane = (b % 2) * BS
            right[b // 2, z, r * BS : (r + 1) * BS, lane : lane + BS] = block
    rights = [Ring(links, "z", lambda s, j=j: right.at[j, s]) for j in range(CHUNKS)]
    rights[0].start()

    lefts = {}
    crossed = []

    def spread(step):
        lefts[step] = Ring(links, "layer", lambda s: left.at[c, over(step), s])
        lefts[step].start()
        cross(step, 0)

    def cross(step, away):
        piece = left.at[c, over(step), lax.rem(x + away, 4)]
        crossed.append(links.copy(piece, piece, "col", 1))

    spread(0)
    y_up.wait_recv()
    spread(3)
    y_down.wait_recv()
    spread(1)
    y_up_pass.wait_recv()
    y_up_far = links.copy(left_pass.at[0], left.at[c, over(3), x, pl.ds(0, 64)], "y", 1)
    y_down_pass.wait_recv()
    y_down_far = links.copy(left_pass.at[1], left.at[c, over(1), x, pl.ds(64, 64)], "y", -1)
    rights[0].forward()
    rights[1].start()
    y_up_far.wait_recv()
    y_down_far.wait_recv()
    spread(2)
    for turn, step in enumerate((0, 3, 1, 2)):
        lefts[step].forward()
        cross(step, 3)
        cross(step, 1)
        if turn < 3:
            rights[turn + 1].forward()
            if turn < 2:
                rights[turn + 2].start()
    for step in (0, 3, 1, 2):
        lefts[step].finish()
        cross(step, 2)
    for made in crossed:
        made.wait_recv()

    def multiply(j, factor):
        def panel(i, carry):
            d = lax.rem(y + jnp.where(i == 0, 2, jnp.where(i == 1, 1, jnp.where(i == 2, 3, 0))), 4)
            total = jnp.zeros((512, WIDE), F32)
            for k in range(2):
                total += jnp.dot(
                    left[k, d].reshape(512, 1024),
                    factor[j, 2 * k : 2 * k + 2].reshape(1024, WIDE),
                    preferred_element_type=F32,
                )
            part[j, i] = total
            return carry

        lax.fori_loop(0, 4, panel, 0)

    class Sums:
        def __init__(self, j, stage):
            self.j, self.slot = j, stage * CHUNKS + j

        def send(self, n, value, step):
            sums_send[self.slot, n] = value.astype(BF16)
            return links.copy(sums_send.at[self.slot, n], sums_recv.at[self.slot, n], "y", step)

        def start(self):
            j = self.j
            self.made = [
                self.send(0, part[j, 0, 0:256], 1),
                self.send(1, part[j, 0, 256:512], -1),
                self.send(2, part[j, 1, 256:512], 1),
                self.send(3, part[j, 2, 0:256], -1),
            ]

        def combine(self):
            j = self.j
            self.made[0].wait_recv()
            self.made.append(self.send(4, part[j, 1, 0:256] + sums_recv[self.slot, 0].astype(F32), 1))
            self.made[1].wait_recv()
            self.made.append(self.send(5, part[j, 2, 256:512] + sums_recv[self.slot, 1].astype(F32), -1))

        def result(self):
            for n in (2, 3, 4, 5):
                self.made[n].wait_recv()
            halves = []
            for h, (a, b) in enumerate(((3, 4), (2, 5))):
                own = part[self.j, 3, h * 256 : (h + 1) * 256]
                halves.append(
                    own + sums_recv[self.slot, a].astype(F32) + sums_recv[self.slot, b].astype(F32)
                )
            return halves

    squares = [Sums(j, 0) for j in range(CHUNKS)]
    cubes = [Sums(j, 1) for j in range(CHUNKS)]
    gathers = [Ring(links, "z", lambda s, j=j: square.at[j, s]) for j in range(CHUNKS)]
    handed = []

    def first(j):
        rights[j].finish()
        multiply(j, right)
        squares[j].start()

    def squared(j):
        for h, value in enumerate(squares[j].result()):
            square[j, z, h * 256 : (h + 1) * 256] = value.astype(BF16)
        gathers[j].start()

    def second(j):
        gathers[j].finish()
        multiply(j, square)
        cubes[j].start()

    def purified(j):
        for h, value in enumerate(cubes[j].result()):
            for r in range(2):
                row = 2 * h + r
                for b in range(2):
                    lanes = slice(b * BS, (b + 1) * BS)
                    own = square[j, z, row * BS : (row + 1) * BS, lanes].astype(F32)
                    block = 3.0 * own - 2.0 * value[r * BS : (r + 1) * BS, lanes]
                    block = jnp.where(kept(row, x * 8 + j * 2 + b), block, jnp.zeros_like(block))
                    pure[j, row, b] = block.astype(BF16)
        where = x * 8 + j * 2
        for step in (1, 2, 3):
            to = lax.rem(x + step, 4)
            handed.append(links.copy(pure.at[j, to], held.at[pl.ds(where, 2)], "layer", step))
        for b in range(2):
            held[where + b] = pure[j, x, b]

    first(0)
    first(1)
    squares[0].combine()
    first(2)
    squares[1].combine()
    squared(0)
    first(3)
    squares[2].combine()
    squared(1)
    gathers[0].forward()
    squares[3].combine()
    second(0)
    squared(2)
    gathers[1].forward()
    cubes[0].combine()
    second(1)
    squared(3)
    gathers[2].forward()
    cubes[1].combine()
    purified(0)
    second(2)
    gathers[3].forward()
    cubes[2].combine()
    purified(1)
    second(3)
    cubes[3].combine()
    purified(2)
    purified(3)
    for made in handed:
        made.wait_recv()
    held_out[...] = held[...]
    for made in links.started:
        made.wait_send()
    assert links.count == COPIES, links.count


def purify(density, pattern):
    return pl.pallas_call(
        purify_kernel,
        out_shape=jax.ShapeDtypeStruct((32, BS, BS), BF16),
        in_specs=[
            pl.BlockSpec(memory_space=pltpu.SMEM),
            pl.BlockSpec(memory_space=pl.ANY),
        ],
        out_specs=pl.BlockSpec(memory_space=pltpu.VMEM),
        scratch_shapes=[
            pltpu.VMEM((BS, 4096), BF16),
            pltpu.VMEM((512, 1024), BF16),
            pltpu.VMEM((2, 4, 4, BS, 1024), BF16),
            pltpu.VMEM((4, BS, 1024), BF16),
            pltpu.VMEM((2, 64, 1024), BF16),
            pltpu.VMEM((CHUNKS, 4, 512, WIDE), BF16),
            pltpu.VMEM((CHUNKS, 4, 512, WIDE), BF16),
            pltpu.VMEM((CHUNKS, 4, 512, WIDE), F32),
            pltpu.VMEM((2 * CHUNKS, 6, 256, WIDE), BF16),
            pltpu.VMEM((2 * CHUNKS, 6, 256, WIDE), BF16),
            pltpu.VMEM((CHUNKS, 4, 2, BS, BS), BF16),
            pltpu.VMEM((32, BS, BS), BF16),
            pltpu.SemaphoreType.DMA((2,)),
            pltpu.SemaphoreType.DMA((COPIES,)),
            pltpu.SemaphoreType.DMA((COPIES,)),
        ],
        compiler_params=pltpu.CompilerParams(
            collective_id=0, has_side_effects=True, vmem_limit_bytes=56 << 20
        ),
    )(pattern, density)


def select(indices, blocks):
    hot = indices[:, None] == jnp.arange(blocks.shape[0], dtype=jnp.int32)[None, :]
    flat = jnp.dot(hot.astype(blocks.dtype), blocks.reshape(blocks.shape[0], BS * BS))
    return flat.reshape(-1, BS, BS)


def shards(density, pattern, holder, slot_index, atom_index, derivative):
    held_blocks = purify(density, pattern)
    holders_total = 32
    capacity = 2
    targets = holder[:, 0]
    entries = jnp.arange(targets.shape[0], dtype=jnp.int32)
    earlier = (targets[:, None] == targets[None, :]) & (entries[None, :] < entries[:, None])
    rank_values = jnp.sum(earlier.astype(jnp.int32), axis=1)
    positions = targets * capacity + rank_values
    position_hot = (
        positions[None, :] == jnp.arange(holders_total * capacity, dtype=jnp.int32)[:, None]
    )
    requests = jnp.sum(jnp.where(position_hot, slot_index[None, :], 0), axis=1).reshape(
        holders_total, capacity
    )
    axes = ("z", "y", "col")
    asked = lax.all_to_all(requests, axes, split_axis=0, concat_axis=0, tiled=True).reshape(-1)
    fetched = select(asked, held_blocks).reshape(holders_total, capacity, BS, BS)
    returned = lax.all_to_all(fetched, axes, split_axis=0, concat_axis=0, tiled=True)
    arrived = select(positions, returned.reshape(holders_total * capacity, BS, BS))
    contrib = jnp.einsum("eij,exij->xe", arrived, derivative, preferred_element_type=jnp.float32)
    atom_hot = (atom_index[:, None] == jnp.arange(ATOM_DEV, dtype=jnp.int32)[None, :]).astype(
        jnp.float32
    )
    return -2.0 * jnp.dot(contrib, atom_hot, precision=lax.Precision.HIGHEST)


def solution(mesh):
    split = Mesh(mesh.devices.reshape(4, 4, 4, 2), ("layer", "z", "y", "col"))
    every = ("layer", "z", "y", "col")
    return jax.shard_map(
        shards,
        mesh=split,
        in_specs=(
            P(("z", "y"), "col"),
            P(("z", "y"), "col"),
            P(every, None),
            P(every),
            P(every),
            P(every, None, None, None),
        ),
        out_specs=P(None, every),
        check_vma=False,
    )
```

time: 422 us -> 211 us (0.50)
  waiting for transfers between devices: 276 us -> 27.8 us
  Pallas kernels: 0 us -> 146 us
  local copies, waits for them, and re-layouts: 46.2 us -> 2.92 us
  matrix products: 41.5 us -> 14.1 us
  blocking collectives: 19.1 us -> 0 us
  between operations: 13.6 us -> 0.09 us
  other arithmetic: 6.7 us -> 2.41 us
    all_gather x4 -> x0, waiting for transfers between devices: 146 us -> none  [the longest x1 49.9 us: purify(): left = lax.all_gather(piece, 'layer', axis=0, tiled=False)]
    pallas_call x0 -> x1, Pallas kernels: none -> 146 us  [purify(): pl.pallas_call(purify_kernel, out_shape=jax.ShapeDtypeStruct((32, BS, BS)...]
    reduce_scatter x2 -> x0, waiting for transfers between devices: 86.5 us -> none  [product(): return lax.psum_scatter(partial, 'y', scatter_dimension=0, tiled=True)]
    dot_general x2 -> x0, matrix products: 27.6 us -> none  [product(): jnp.dot(left, factor, preferred_element_type=jnp.float32).astype(bf)]
    unnamed x13 -> x6, local copies, waits for them, and re-layouts: 19.5 us -> 0.01 us
    all_to_all x1 -> x0, blocking collectives: 19.1 us -> none  [purify(): piece = lax.all_to_all(piece, 'y', 0, 0, tiled=True)]
    transpose x3 -> x0, local copies, waits for them, and re-layouts: 17.6 us -> none  [the longest x1 16.5 us: purify(): left = left.transpose(2, 1, 3, 0, 4).reshape(2048, 2048)]
    all_to_all x1 -> x0, waiting for transfers between devices: 14.7 us -> none  [purify(): return lax.all_to_all(blocks, 'layer', 0, 0, tiled=True).reshape(32, BS, BS)]
  transfers between devices with their start and end apart: 9 -> 2, of which waited for: 8 -> 1; matrix products, arithmetic and copies ran while one was open for 8% -> 0% of each run, Pallas kernels for 0% -> 70%
where the time goes in v2:
time: 211 us; the launch traced here: 210 us
  Pallas kernels  146 us (69%)
  waiting for transfers between devices  27.8 us (13%)
  starting transfers between devices  16.5 us (8%)
  matrix products  14.1 us (7%)
  local copies, waits for them, and re-layouts  2.92 us (1%)
  other arithmetic  2.41 us (1%)
    pallas_call x1, Pallas kernels, purify(): pl.pallas_call(purify_kernel, out_shape=jax.ShapeDtypeStruct((32, BS, BS)...  146 us
    all_to_all x1, waiting for transfers between devices, shards(): lax.all_to_all(fetched, axes, split_axis=0, concat_axis=0, tiled=True)  27.8 us
    all_to_all x1, starting transfers between devices, shards(): lax.all_to_all(requests, axes, split_axis=0, concat_axis=0, tiled=True)  9.6 us
    dot_general x1, matrix products, shards(): jnp.einsum('eij,exij->xe', arrived, derivative, preferred_element_type=jn...  8 us
    all_to_all x1, starting transfers between devices, shards(): lax.all_to_all(fetched, axes, split_axis=0, concat_axis=0, tiled=True)  6.86 us
    dot_general x2, matrix products, select(): jnp.dot(hot.astype(blocks.dtype), blocks.reshape(blocks.shape[0], BS * BS))  5.26 us
  transfers between devices with their start and end apart: 2, of which 1 were waited for; matrix products, arithmetic and copies ran while one was open for 0% of the time, Pallas kernels for 70%

profile of v2, /device:TPU:1, one launch (start us, length us, event | category | flops | bytes accessed | tf_op | source)
XLA Modules:
  0.0 209.6 jit_solution(7854382199684688308)
XLA Ops:
  0.0 0.0 copy-start
  0.0 1.0 convert_reduce_fusion
  1.0 0.7 multiply_add_fusion
  1.7 0.7 select_reduce_fusion
  2.4 0.7 all_to_all.9
  3.1 9.6 %all-to-all-start = ((s32[32,1,2]{2,1,0:T(1,128)}), s32[32,1,2]{2,1,0:T(1,128)S(1)}, u32[]{:S(2)}, u32[]{:S(2)}) async-start(s32[32,1,2]{2,1,0:T(1,128)} %bitcast.4), calls=%async_computation | async-start | bytes 32768 | tf_op jit(solution)/shard_map/all_to_all | solution.py:340
  12.7 145.9 %shard_map.64 = bf16[32,128,128]{2,1,0:T(8,128)(2,1)} custom-call(s32[4,32]{1,0:T(4,128)} %pattern.1, bf16[512,4096]{1,0:T(8,128)(2,1)} %density.1), custom_call_target="tpu_custom_call" | custom-call | tf_op jit(solution)/shard_map/pallas_call | solution.py:287
  158.6 0.0 all-to-all-done
  158.6 0.1 copy.21
  158.7 2.2 %fusion.9 = bf16[32,2,128,128]{3,0,2,1:T(8,128)(2,1)S(1)} fusion(s32[32,2]{0,1:T(2,128)S(1)} %bitcast.58, bf16[4,8,128,128]{3,2,1,0:T(8,128)(2,1)} %bitcast.57), kind=kOutput, calls=%fused_computation.11 | convolution fusion | flops 67110912 | bytes 3145984 | tf_op jit(solution)/shard_map/dot_general | solution.py:320
  160.9 2.1 %copy.23 = bf16[32,2,128,128]{3,2,1,0:T(8,128)(2,1)} copy(bf16[32,2,128,128]{3,0,2,1:T(8,128)(2,1)S(1)} %fusion.9) | data formatting | bytes 4194304 | tf_op jit(solution)/shard_map/dot_general | solution.py:320
  163.0 0.0 copy-start.1
  163.0 6.9 %all-to-all-start.1 = ((bf16[32,2,128,128]{3,2,1,0:T(8,128)(2,1)}), bf16[32,2,128,128]{3,2,1,0:T(8,128)(2,1)}, u32[]{:S(2)}, u32[]{:S(2)}) async-start(bf16[32,2,128,128]{3,2,1,0:T(8,128)(2,1)} %copy.23), calls=%async_computation.1 | async-start | bytes 4194304 | tf_op jit(solution)/shard_map/all_to_all | solution.py:342
  169.9 0.0 copy-done.1
  169.9 27.8 %all-to-all-done.1 = bf16[32,2,128,128]{3,2,1,0:T(8,128)(2,1)} async-done(((bf16[32,2,128,128]{3,2,1,0:T(8,128)(2,1)}), bf16[32,2,128,128]{3,2,1,0:T(8,128)(2,1)}, u32[]{:S(2)}, u32[]{:S(2)}) %all-to-all-start.1) | async-done | bytes 2097184 | tf_op jit(solution)/shard_map/all_to_all | solution.py:342
  197.7 3.1 %fusion.6 = bf16[32,128,128,1]{2,0,1,3:T(8,128)(2,1)S(1)} fusion(s32[32]{0:T(128)S(1)} %fusion.19, bf16[8,8,128,128]{3,2,1,0:T(8,128)(2,1)} %bitcast.24), kind=kOutput, calls=%fused_computation.7 | convolution fusion | flops 67110912 | bytes 3145856 | tf_op jit(solution)/shard_map/dot_general | solution.py:320
  200.8 0.0 copy-done
  200.8 0.0 copy-start.2
  200.8 8.0 %fusion = f32[32,1,3,1]{2,1,3,0:T(1,128)S(1)} fusion(bf16[32,3,128,128]{3,2,1,0:T(8,128)(2,1)S(1)} %copy-done, bf16[32,128,128,1]{2,0,1,3:T(8,128)(2,1)S(1)} %fusion.6), kind=kOutput, calls=%fused_computation | convolution fusion | flops 3145728 | bytes 4194688 | tf_op jit(solution)/shard_map/eij,exij->xe/dot_general | solution.py:344
  208.8 0.0 copy-done.2
  208.8 0.8 convolution_multiply_fusion
  (1 shorter events, 0.0 us)
Async XLA Ops:
  0.0 200.8 %copy-start = (bf16[32,3,128,128]{3,2,1,0:T(8,128)(2,1)S(1)}, bf16[32,3,128,128]{3,2,1,0:T(8,128)(2,1)}, u32[]{:S(2)}) copy-start(bf16[32,3,128,128]{3,2,1,0:T(8,128)(2,1)} %param.11) | copy-start | bytes 9437188
  3.1 155.5 %all-to-all-start = ((s32[32,1,2]{2,1,0:T(1,128)}), s32[32,1,2]{2,1,0:T(1,128)S(1)}, u32[]{:S(2)}, u32[]{:S(2)}) async-start(s32[32,1,2]{2,1,0:T(1,128)} %bitcast.4), calls=%async_computation | async-start | bytes 32768 | tf_op jit(solution)/shard_map/all_to_all | solution.py:340
  163.0 6.9 %copy-start.1 = (s32[32,1]{0,1:T(1,128)S(1)}, s32[32,1]{0,1:T(1,128)}, u32[]{:S(2)}) copy-start(s32[32,1]{0,1:T(1,128)} %param.8) | copy-start | bytes 388
  163.0 34.7 %all-to-all-start.1 = ((bf16[32,2,128,128]{3,2,1,0:T(8,128)(2,1)}), bf16[32,2,128,128]{3,2,1,0:T(8,128)(2,1)}, u32[]{:S(2)}, u32[]{:S(2)}) async-start(bf16[32,2,128,128]{3,2,1,0:T(8,128)(2,1)} %copy.23), calls=%async_computation.1 | async-start | bytes 4194304 | tf_op jit(solution)/shard_map/all_to_all | solution.py:342
  200.8 8.0 %copy-start.2 = (s32[32]{0:T(128)S(1)}, s32[32]{0:T(128)}, u32[]{:S(2)}) copy-start(s32[32]{0:T(128)} %param.10) | copy-start | bytes 388

commit v3 on v2

--- a/solution.py
+++ b/solution.py
@@ -12,7 +12,7 @@
 F32 = jnp.float32
 BF16 = jnp.bfloat16
 MESH = pl.DeviceIdType.MESH
-COPIES = 130
+COPIES = 192
 
 
 class Links:
@@ -22,14 +22,17 @@
         self.count = 0
 
     def copy(self, src, dst, axis, step):
+        length = 2 if axis == "col" else 4
+        return self.to(src, dst, {axis: lax.rem(self.place[axis] + step + length, length)})
+
+    def to(self, src, dst, device):
         number, self.count = self.count, self.count + 1
-        length = 2 if axis == "col" else 4
         made = pltpu.make_async_remote_copy(
             src_ref=src,
             dst_ref=dst,
             send_sem=self.send_sems.at[number],
             recv_sem=self.recv_sems.at[number],
-            device_id={axis: lax.rem(self.place[axis] + step + length, length)},
+            device_id=device,
             device_id_type=MESH,
         )
         made.start()
@@ -62,8 +65,9 @@
 
 
 def purify_kernel(
-    pattern, density, held_out,
+    pattern, density, targets_col, targets_row, slots_row, atoms_col, derivative, forces,
     rows_in, cols_in, left, left_send, left_pass, right, square, part, sums_send, sums_recv, pure, held,
+    der, asked_send, asked_recv, asked_rows, spots, asked, spot_of, picked, arrived, contrib,
     in_sems, send_sems, recv_sems,
 ):
     x, z, y, c = (lax.axis_index(a) for a in ("layer", "z", "y", "col"))
@@ -77,16 +81,36 @@
     )
     load_rows.start()
     load_cols.start()
+    load_der = pltpu.make_async_copy(derivative, der, in_sems.at[2])
+    load_der.start()
     barrier = pltpu.get_barrier_semaphore()
-    greeted = 0
-    for axis, steps in (("y", (1, 3)), ("z", (1, 3)), ("layer", (1, 2, 3)), ("col", (1,))):
-        length = 2 if axis == "col" else 4
-        for step in steps:
-            pl.semaphore_signal(
-                barrier, inc=1, device_id={axis: lax.rem(place[axis] + step, length)},
-                device_id_type=MESH,
-            )
-            greeted += 1
+    others = [(dz, dy, dc) for dz in (2, 1, 3, 0) for dy in (2, 1, 3, 0) for dc in (0, 1)][:-2]
+    others.append((0, 0, 1))
+
+    def device(dz, dy, dc):
+        return {"z": lax.rem(z + dz, 4), "y": lax.rem(y + dy, 4), "col": lax.rem(c + dc, 2)}
+
+    def holder_of(at):
+        return at["z"] * 8 + at["y"] * 2 + at["col"]
+
+    me = z * 8 + y * 2 + c
+    greeted = [device(*d) for d in others] + [{"layer": lax.rem(x + step, 4)} for step in (1, 2, 3)]
+    for at in greeted:
+        pl.semaphore_signal(barrier, inc=1, device_id=at, device_id_type=MESH)
+
+    across = lax.broadcasted_iota(jnp.int32, (32, 32), 1)
+    down = lax.broadcasted_iota(jnp.int32, (32, 32), 0)
+    earlier = (targets_col[...] == targets_row[...]) & (down < across)
+    spot = 2 * targets_row[...] + jnp.sum(jnp.where(earlier, 1, 0), axis=0, keepdims=True)
+    spots[...] = jnp.zeros_like(spots)
+    spots[0:1, 0:32] = spot
+    lane = lax.broadcasted_iota(jnp.int32, (32, BS), 1)
+    table = jnp.zeros((32, BS), jnp.int32)
+    for k in range(2):
+        mine = jnp.where(spot == 2 * down + k, slots_row[...], 0)
+        table = jnp.where(lane == k, jnp.sum(mine, axis=1, keepdims=True), table)
+    asked_send[...] = jnp.broadcast_to(table[:, None, :], asked_send.shape)
+    asked_recv[me] = asked_send[me]
 
     def kept(row_block, col_block):
         inside = pattern[row_block, col_block] == 1
@@ -99,7 +123,7 @@
         lane = (b // 16) * 512 + (b % 4) * BS
         left_send[(b % 16) // 4, :, lane : lane + BS] = block
     left[c, y, x] = left_send[y]
-    pl.semaphore_wait(barrier, greeted)
+    pl.semaphore_wait(barrier, len(greeted))
 
     def over(step):
         return lax.rem(y + step, 4)
@@ -117,6 +141,10 @@
             block = jnp.where(kept(r, x * 8 + b), block, jnp.zeros_like(block))
             lane = (b % 2) * BS
             right[b // 2, z, r * BS : (r + 1) * BS, lane : lane + BS] = block
+    requests = []
+    for d in others:
+        at = device(*d)
+        requests.append(links.to(asked_send.at[holder_of(at)], asked_recv.at[me], at))
     rights = [Ring(links, "z", lambda s, j=j: right.at[j, s]) for j in range(CHUNKS)]
     rights[0].start()
 
@@ -247,8 +275,19 @@
         for b in range(2):
             held[where + b] = pure[j, x, b]
 
+    for made in requests:
+        made.wait_recv()
+    asked_rows[...] = asked_recv[:, 0, :]
+    tables = [
+        pltpu.make_async_copy(asked_rows, asked, in_sems.at[3]),
+        pltpu.make_async_copy(spots, spot_of, in_sems.at[4]),
+    ]
+    for made in tables:
+        made.start()
     first(0)
     first(1)
+    for made in tables:
+        made.wait()
     squares[0].combine()
     first(2)
     squares[1].combine()
@@ -277,21 +316,50 @@
     purified(3)
     for made in handed:
         made.wait_recv()
-    held_out[...] = held[...]
+    fetches = []
+    for d in others:
+        at = device(*d)
+        to = holder_of(at)
+        for k in range(2):
+            picked[to, k] = held[asked[to, k]]
+        fetches.append(links.to(picked.at[to], arrived.at[pl.ds(2 * me, 2)], at))
+    for k in range(2):
+        arrived[2 * me + k] = held[asked[me, k]]
+    load_der.wait()
+    for made in fetches:
+        made.wait_recv()
+
+    def contract(e, carry):
+        block = arrived[spot_of[0, e]].astype(F32)
+        for k in range(3):
+            terms = block * der[e, k].astype(F32)
+            contrib[k, e] = jnp.sum(terms.reshape(16, 8, BS), axis=0)
+        return carry
+
+    lax.fori_loop(0, 32, contract, 0)
+    atoms = lax.broadcasted_iota(jnp.int32, (32, ATOM_DEV), 1)
+    atom_hot = jnp.where(atoms_col[...] == atoms, 1.0, 0.0).astype(F32)
+    for k in range(3):
+        lanes = jnp.sum(contrib[k], axis=1)
+        terms = lax.dot_general(
+            jnp.ones((8, BS), F32), lanes, (((1,), (1,)), ((), ())),
+            precision=lax.Precision.HIGHEST, preferred_element_type=F32,
+        )
+        summed = jnp.dot(terms, atom_hot, precision=lax.Precision.HIGHEST, preferred_element_type=F32)
+        forces[k : k + 1, :] = -2.0 * summed[0:1, :]
     for made in links.started:
         made.wait_send()
     assert links.count == COPIES, links.count
 
 
-def purify(density, pattern):
+def shards(density, pattern, holder, slot_index, atom_index, derivative):
+    vmem = pl.BlockSpec(memory_space=pltpu.VMEM)
+    hbm = pl.BlockSpec(memory_space=pl.ANY)
     return pl.pallas_call(
         purify_kernel,
-        out_shape=jax.ShapeDtypeStruct((32, BS, BS), BF16),
-        in_specs=[
-            pl.BlockSpec(memory_space=pltpu.SMEM),
-            pl.BlockSpec(memory_space=pl.ANY),
-        ],
-        out_specs=pl.BlockSpec(memory_space=pltpu.VMEM),
+        out_shape=jax.ShapeDtypeStruct((3, ATOM_DEV), F32),
+        in_specs=[pl.BlockSpec(memory_space=pltpu.SMEM), hbm, vmem, vmem, vmem, vmem, hbm],
+        out_specs=vmem,
         scratch_shapes=[
             pltpu.VMEM((BS, 4096), BF16),
             pltpu.VMEM((512, 1024), BF16),
@@ -305,47 +373,27 @@
             pltpu.VMEM((2 * CHUNKS, 6, 256, WIDE), BF16),
             pltpu.VMEM((CHUNKS, 4, 2, BS, BS), BF16),
             pltpu.VMEM((32, BS, BS), BF16),
-            pltpu.SemaphoreType.DMA((2,)),
+            pltpu.VMEM((32, 3, BS, BS), BF16),
+            pltpu.VMEM((32, 8, BS), jnp.int32),
+            pltpu.VMEM((32, 8, BS), jnp.int32),
+            pltpu.VMEM((32, BS), jnp.int32),
+            pltpu.VMEM((8, BS), jnp.int32),
+            pltpu.SMEM((32, BS), jnp.int32),
+            pltpu.SMEM((8, BS), jnp.int32),
+            pltpu.VMEM((32, 2, BS, BS), BF16),
+            pltpu.VMEM((64, BS, BS), BF16),
+            pltpu.VMEM((3, 32, 8, BS), F32),
+            pltpu.SemaphoreType.DMA((5,)),
             pltpu.SemaphoreType.DMA((COPIES,)),
             pltpu.SemaphoreType.DMA((COPIES,)),
         ],
         compiler_params=pltpu.CompilerParams(
-            collective_id=0, has_side_effects=True, vmem_limit_bytes=56 << 20
+            collective_id=0, has_side_effects=True, vmem_limit_bytes=60 << 20
         ),
-    )(pattern, density)
-
-
-def select(indices, blocks):
-    hot = indices[:, None] == jnp.arange(blocks.shape[0], dtype=jnp.int32)[None, :]
-    flat = jnp.dot(hot.astype(blocks.dtype), blocks.reshape(blocks.shape[0], BS * BS))
-    return flat.reshape(-1, BS, BS)
-
-
-def shards(density, pattern, holder, slot_index, atom_index, derivative):
-    held_blocks = purify(density, pattern)
-    holders_total = 32
-    capacity = 2
-    targets = holder[:, 0]
-    entries = jnp.arange(targets.shape[0], dtype=jnp.int32)
-    earlier = (targets[:, None] == targets[None, :]) & (entries[None, :] < entries[:, None])
-    rank_values = jnp.sum(earlier.astype(jnp.int32), axis=1)
-    positions = targets * capacity + rank_values
-    position_hot = (
-        positions[None, :] == jnp.arange(holders_total * capacity, dtype=jnp.int32)[:, None]
+    )(
+        pattern, density, holder, holder.reshape(1, 32), slot_index.reshape(1, 32),
+        atom_index.reshape(32, 1), derivative,
     )
-    requests = jnp.sum(jnp.where(position_hot, slot_index[None, :], 0), axis=1).reshape(
-        holders_total, capacity
-    )
-    axes = ("z", "y", "col")
-    asked = lax.all_to_all(requests, axes, split_axis=0, concat_axis=0, tiled=True).reshape(-1)
-    fetched = select(asked, held_blocks).reshape(holders_total, capacity, BS, BS)
-    returned = lax.all_to_all(fetched, axes, split_axis=0, concat_axis=0, tiled=True)
-    arrived = select(positions, returned.reshape(holders_total * capacity, BS, BS))
-    contrib = jnp.einsum("eij,exij->xe", arrived, derivative, preferred_element_type=jnp.float32)
-    atom_hot = (atom_index[:, None] == jnp.arange(ATOM_DEV, dtype=jnp.int32)[None, :]).astype(
-        jnp.float32
-    )
-    return -2.0 * jnp.dot(contrib, atom_hot, precision=lax.Precision.HIGHEST)
 
 
 def solution(mesh):

time: 211 us -> 184 us (0.87)
  Pallas kernels: 146 us -> 180 us
  waiting for transfers between devices: 27.8 us -> 0 us
  starting transfers between devices: 16.5 us -> 0 us
  matrix products: 14.1 us -> 0 us
  other arithmetic: 2.41 us -> 0 us
    pallas_call x1, Pallas kernels: 146 us -> 180 us  [shards(): pl.pallas_call(purify_kernel, out_shape=jax.ShapeDtypeStruct((3, ATOM_DEV...]
    all_to_all x2 -> x0, waiting for transfers between devices: 27.8 us -> none  [the longest x1 27.8 us: shards(): lax.all_to_all(fetched, axes, split_axis=0, concat_axis=0, tiled=True)]
    all_to_all x2 -> x0, starting transfers between devices: 16.5 us -> none  [the longest x1 9.6 us: shards(): lax.all_to_all(requests, axes, split_axis=0, concat_axis=0, tiled=True)]
    dot_general x4 -> x0, matrix products: 14.1 us -> none  [the longest x1 8 us: shards(): jnp.einsum('eij,exij->xe', arrived, derivative, preferred_element_type=jn...]
    unnamed x6 -> x2, local copies, waits for them, and re-layouts: 0.01 us -> 2.56 us
    dot_general x1 -> x0, local copies, waits for them, and re-layouts: 2.11 us -> none  [select(): jnp.dot(hot.astype(blocks.dtype), blocks.reshape(blocks.shape[0], BS * BS))]
  transfers between devices with their start and end apart: 2 -> 0, of which waited for: 1 -> 0; matrix products, arithmetic and copies ran while one was open for 0% -> 0% of each run, Pallas kernels for 70% -> 0%
where the time goes in v3:
time: 184 us
  Pallas kernels  180 us (98%)
  local copies, waits for them, and re-layouts  3.89 us (2%)
    pallas_call x1, Pallas kernels, shards(): pl.pallas_call(purify_kernel, out_shape=jax.ShapeDtypeStruct((3, ATOM_DEV...  180 us

profile of v3, /device:TPU:1, one launch (start us, length us, event | category | flops | bytes accessed | tf_op | source)
XLA Modules:
  0.0 184.1 jit_solution(6700623269458263845)
XLA Ops:
  0.0 1.3 copy.8.atoms_col
  1.3 1.3 copy.7.targets_col
  2.7 180.2 %shard_map.64 = f32[3,8]{1,0:T(4,128)} custom-call(s32[4,32]{1,0:T(4,128)} %pattern.1, bf16[512,4096]{1,0:T(8,128)(2,1)} %density.1, s32[32,1]{1,0:T(8,128)} %copy.7.targets_col, s32[1,32]{1,0:T(1,128)} %bitcast.3, s32[1,32]{1,0:T(1,128)} %bitcast.4, s32[32,1]{1,0:T(8,128)} %copy.8.atoms_col, bf16[32,3,128,128]{3,2,1,0:T(8,128)(2,1)} %derivative.1), custom_call_target="tpu_custom_call" | custom-call | tf_op jit(solution)/shard_map/pallas_call | solution.py:358
  182.9 1.2 copy.10

commit v4 on v3

--- a/solution.py
+++ b/solution.py
@@ -12,7 +12,7 @@
 F32 = jnp.float32
 BF16 = jnp.bfloat16
 MESH = pl.DeviceIdType.MESH
-COPIES = 192
+COPIES = 182
 
 
 class Links:
@@ -65,8 +65,8 @@
 
 
 def purify_kernel(
-    pattern, density, targets_col, targets_row, slots_row, atoms_col, derivative, forces,
-    rows_in, cols_in, left, left_send, left_pass, right, square, part, sums_send, sums_recv, pure, held,
+    pattern, density, targets_row, slots_row, atoms_row, derivative, forces,
+    rows_in, cols_in, own_in, left, left_send, right, square, part, sums_send, sums_recv, pure, held,
     der, asked_send, asked_recv, asked_rows, spots, asked, spot_of, picked, arrived, contrib,
     in_sems, send_sems, recv_sems,
 ):
@@ -81,6 +81,15 @@
     )
     load_rows.start()
     load_cols.start()
+    load_own = [
+        pltpu.make_async_copy(
+            density.at[:, pl.ds(pl.multiple_of(h * 2048 + y * 512, 512), 512)],
+            own_in.at[h], in_sems.at[5 + h],
+        )
+        for h in range(2)
+    ]
+    for made in load_own:
+        made.start()
     load_der = pltpu.make_async_copy(derivative, der, in_sems.at[2])
     load_der.start()
     barrier = pltpu.get_barrier_semaphore()
@@ -100,7 +109,11 @@
 
     across = lax.broadcasted_iota(jnp.int32, (32, 32), 1)
     down = lax.broadcasted_iota(jnp.int32, (32, 32), 0)
-    earlier = (targets_col[...] == targets_row[...]) & (down < across)
+
+    def column(row):
+        return jnp.sum(jnp.where(down == across, row, 0), axis=1, keepdims=True)
+
+    earlier = (column(targets_row[...]) == targets_row[...]) & (down < across)
     spot = 2 * targets_row[...] + jnp.sum(jnp.where(earlier, 1, 0), axis=0, keepdims=True)
     spots[...] = jnp.zeros_like(spots)
     spots[0:1, 0:32] = spot
@@ -122,17 +135,15 @@
         block = jnp.where(kept(x, b), block, jnp.zeros_like(block))
         lane = (b // 16) * 512 + (b % 4) * BS
         left_send[(b % 16) // 4, :, lane : lane + BS] = block
-    left[c, y, x] = left_send[y]
     pl.semaphore_wait(barrier, len(greeted))
 
     def over(step):
         return lax.rem(y + step, 4)
 
-    y_up = links.copy(left_send.at[over(1)], left.at[c, y, x], "y", 1)
-    y_down = links.copy(left_send.at[over(3)], left.at[c, y, x], "y", -1)
-    far = left_send.at[over(2)]
-    y_up_pass = links.copy(far.at[pl.ds(0, 64)], left_pass.at[0], "y", 1)
-    y_down_pass = links.copy(far.at[pl.ds(64, 64)], left_pass.at[1], "y", -1)
+    brought = {
+        step: links.copy(left_send.at[over(-step % 4)], left.at[c, y, x], "y", -step)
+        for step in (3, 1, 2)
+    }
 
     load_cols.wait()
     for b in range(8):
@@ -148,48 +159,45 @@
     rights = [Ring(links, "z", lambda s, j=j: right.at[j, s]) for j in range(CHUNKS)]
     rights[0].start()
 
+    for made in load_own:
+        made.wait()
+    for h in range(2):
+        for r in range(4):
+            for w in range(4):
+                block = own_in[h, r * BS : (r + 1) * BS, w * BS : (w + 1) * BS]
+                block = jnp.where(kept(r, h * 16 + y * 4 + w), block, jnp.zeros_like(block))
+                lane = h * 512 + w * BS
+                left[c, y, r, :, lane : lane + BS] = block
+    crossed = {0: [links.copy(left.at[c, y], left.at[c, y], "col", 1)], 1: [], 2: [], 3: []}
     lefts = {}
-    crossed = []
+
+    def cross(step, away):
+        piece = left.at[c, over(step), lax.rem(x + away, 4)]
+        crossed[step].append(links.copy(piece, piece, "col", 1))
 
     def spread(step):
+        brought[step].wait_recv()
         lefts[step] = Ring(links, "layer", lambda s: left.at[c, over(step), s])
         lefts[step].start()
         cross(step, 0)
 
-    def cross(step, away):
-        piece = left.at[c, over(step), lax.rem(x + away, 4)]
-        crossed.append(links.copy(piece, piece, "col", 1))
-
-    spread(0)
-    y_up.wait_recv()
-    spread(3)
-    y_down.wait_recv()
-    spread(1)
-    y_up_pass.wait_recv()
-    y_up_far = links.copy(left_pass.at[0], left.at[c, over(3), x, pl.ds(0, 64)], "y", 1)
-    y_down_pass.wait_recv()
-    y_down_far = links.copy(left_pass.at[1], left.at[c, over(1), x, pl.ds(64, 64)], "y", -1)
-    rights[0].forward()
-    rights[1].start()
-    y_up_far.wait_recv()
-    y_down_far.wait_recv()
-    spread(2)
-    for turn, step in enumerate((0, 3, 1, 2)):
+    def relay(step):
         lefts[step].forward()
         cross(step, 3)
         cross(step, 1)
-        if turn < 3:
-            rights[turn + 1].forward()
-            if turn < 2:
-                rights[turn + 2].start()
-    for step in (0, 3, 1, 2):
+
+    def gathered(step):
         lefts[step].finish()
         cross(step, 2)
-    for made in crossed:
-        made.wait_recv()
-
-    def multiply(j, factor):
-        def panel(i, carry):
+
+    def complete(*steps):
+        for step in steps:
+            for made in crossed[step]:
+                made.wait_recv()
+
+    def multiply(j, factor, panels):
+        def panel(turn, carry):
+            i = jnp.where(turn == 0, panels[0], panels[1])
             d = lax.rem(y + jnp.where(i == 0, 2, jnp.where(i == 1, 1, jnp.where(i == 2, 3, 0))), 4)
             total = jnp.zeros((512, WIDE), F32)
             for k in range(2):
@@ -201,31 +209,34 @@
             part[j, i] = total
             return carry
 
-        lax.fori_loop(0, 4, panel, 0)
+        lax.fori_loop(0, 2, panel, 0)
 
     class Sums:
         def __init__(self, j, stage):
-            self.j, self.slot = j, stage * CHUNKS + j
+            self.j, self.slot, self.made = j, stage * CHUNKS + j, {}
 
         def send(self, n, value, step):
             sums_send[self.slot, n] = value.astype(BF16)
             return links.copy(sums_send.at[self.slot, n], sums_recv.at[self.slot, n], "y", step)
 
-        def start(self):
+        def far(self, factor):
             j = self.j
-            self.made = [
-                self.send(0, part[j, 0, 0:256], 1),
-                self.send(1, part[j, 0, 256:512], -1),
-                self.send(2, part[j, 1, 256:512], 1),
-                self.send(3, part[j, 2, 0:256], -1),
-            ]
+            multiply(j, factor, (0, 3))
+            self.made[0] = self.send(0, part[j, 0, 0:256], 1)
+            self.made[1] = self.send(1, part[j, 0, 256:512], -1)
+
+        def near(self, factor):
+            j = self.j
+            multiply(j, factor, (1, 2))
+            self.made[2] = self.send(2, part[j, 1, 256:512], 1)
+            self.made[3] = self.send(3, part[j, 2, 0:256], -1)
 
         def combine(self):
             j = self.j
             self.made[0].wait_recv()
-            self.made.append(self.send(4, part[j, 1, 0:256] + sums_recv[self.slot, 0].astype(F32), 1))
+            self.made[4] = self.send(4, part[j, 1, 0:256] + sums_recv[self.slot, 0].astype(F32), 1)
             self.made[1].wait_recv()
-            self.made.append(self.send(5, part[j, 2, 256:512] + sums_recv[self.slot, 1].astype(F32), -1))
+            self.made[5] = self.send(5, part[j, 2, 256:512] + sums_recv[self.slot, 1].astype(F32), -1)
 
         def result(self):
             for n in (2, 3, 4, 5):
@@ -243,11 +254,6 @@
     gathers = [Ring(links, "z", lambda s, j=j: square.at[j, s]) for j in range(CHUNKS)]
     handed = []
 
-    def first(j):
-        rights[j].finish()
-        multiply(j, right)
-        squares[j].start()
-
     def squared(j):
         for h, value in enumerate(squares[j].result()):
             square[j, z, h * 256 : (h + 1) * 256] = value.astype(BF16)
@@ -255,8 +261,8 @@
 
     def second(j):
         gathers[j].finish()
-        multiply(j, square)
-        cubes[j].start()
+        cubes[j].far(square)
+        cubes[j].near(square)
 
     def purified(j):
         for h, value in enumerate(cubes[j].result()):
@@ -275,6 +281,13 @@
         for b in range(2):
             held[where + b] = pure[j, x, b]
 
+    spread(3)
+    spread(1)
+    rights[0].forward()
+    rights[1].start()
+    spread(2)
+    relay(3)
+    relay(1)
     for made in requests:
         made.wait_recv()
     asked_rows[...] = asked_recv[:, 0, :]
@@ -284,15 +297,34 @@
     ]
     for made in tables:
         made.start()
-    first(0)
-    first(1)
+    gathered(3)
+    gathered(1)
+    rights[1].forward()
+    rights[2].start()
+    relay(2)
     for made in tables:
         made.wait()
+    rights[0].finish()
+    complete(0, 3, 1)
+    squares[0].near(right)
+    gathered(2)
+    rights[1].finish()
+    squares[1].near(right)
+    rights[2].forward()
+    rights[3].start()
+    complete(2)
+    squares[0].far(right)
+    squares[1].far(right)
     squares[0].combine()
-    first(2)
+    rights[2].finish()
+    squares[2].far(right)
+    squares[2].near(right)
     squares[1].combine()
     squared(0)
-    first(3)
+    rights[3].forward()
+    rights[3].finish()
+    squares[3].far(right)
+    squares[3].near(right)
     squares[2].combine()
     squared(1)
     gathers[0].forward()
@@ -338,7 +370,7 @@
 
     lax.fori_loop(0, 32, contract, 0)
     atoms = lax.broadcasted_iota(jnp.int32, (32, ATOM_DEV), 1)
-    atom_hot = jnp.where(atoms_col[...] == atoms, 1.0, 0.0).astype(F32)
+    atom_hot = jnp.where(column(atoms_row[...]) == atoms, 1.0, 0.0).astype(F32)
     for k in range(3):
         lanes = jnp.sum(contrib[k], axis=1)
         terms = lax.dot_general(
@@ -358,14 +390,14 @@
     return pl.pallas_call(
         purify_kernel,
         out_shape=jax.ShapeDtypeStruct((3, ATOM_DEV), F32),
-        in_specs=[pl.BlockSpec(memory_space=pltpu.SMEM), hbm, vmem, vmem, vmem, vmem, hbm],
+        in_specs=[pl.BlockSpec(memory_space=pltpu.SMEM), hbm, vmem, vmem, vmem, hbm],
         out_specs=vmem,
         scratch_shapes=[
             pltpu.VMEM((BS, 4096), BF16),
             pltpu.VMEM((512, 1024), BF16),
+            pltpu.VMEM((2, 512, 512), BF16),
             pltpu.VMEM((2, 4, 4, BS, 1024), BF16),
             pltpu.VMEM((4, BS, 1024), BF16),
-            pltpu.VMEM((2, 64, 1024), BF16),
             pltpu.VMEM((CHUNKS, 4, 512, WIDE), BF16),
             pltpu.VMEM((CHUNKS, 4, 512, WIDE), BF16),
             pltpu.VMEM((CHUNKS, 4, 512, WIDE), F32),
@@ -383,7 +415,7 @@
             pltpu.VMEM((32, 2, BS, BS), BF16),
             pltpu.VMEM((64, BS, BS), BF16),
             pltpu.VMEM((3, 32, 8, BS), F32),
-            pltpu.SemaphoreType.DMA((5,)),
+            pltpu.SemaphoreType.DMA((7,)),
             pltpu.SemaphoreType.DMA((COPIES,)),
             pltpu.SemaphoreType.DMA((COPIES,)),
         ],
@@ -391,8 +423,8 @@
             collective_id=0, has_side_effects=True, vmem_limit_bytes=60 << 20
         ),
     )(
-        pattern, density, holder, holder.reshape(1, 32), slot_index.reshape(1, 32),
-        atom_index.reshape(32, 1), derivative,
+        pattern, density, holder.reshape(1, 32), slot_index.reshape(1, 32),
+        atom_index.reshape(1, 32), derivative,
     )
 
 

time: 184 us -> 159 us (0.86)
  Pallas kernels: 180 us -> 157 us
  local copies, waits for them, and re-layouts: 3.89 us -> 1.26 us
    pallas_call x1, Pallas kernels: 180 us -> 157 us  [shards(): pl.pallas_call(purify_kernel, out_shape=jax.ShapeDtypeStruct((3, ATOM_DEV...]
where the time goes in v4:
time: 159 us
  Pallas kernels  157 us (99%)
    pallas_call x1, Pallas kernels, shards(): pl.pallas_call(purify_kernel, out_shape=jax.ShapeDtypeStruct((3, ATOM_DEV...  157 us

profile of v4, /device:TPU:1, one launch (start us, length us, event | category | flops | bytes accessed | tf_op | source)
XLA Modules:
  0.0 158.6 jit_solution(8800768794267269281)
XLA Ops:
  0.0 157.4 %shard_map.64 = f32[3,8]{1,0:T(4,128)} custom-call(s32[4,32]{1,0:T(4,128)} %pattern.1, bf16[512,4096]{1,0:T(8,128)(2,1)} %density.1, s32[1,32]{1,0:T(1,128)} %bitcast.3, s32[1,32]{1,0:T(1,128)} %bitcast.4, s32[1,32]{1,0:T(1,128)} %bitcast.5, bf16[32,3,128,128]{3,2,1,0:T(8,128)(2,1)} %derivative.1), custom_call_target="tpu_custom_call" | custom-call | tf_op jit(solution)/shard_map/pallas_call | solution.py:390
  157.4 1.3 copy.8

commit v5 on v4

--- a/solution.py
+++ b/solution.py
@@ -12,7 +12,7 @@
 F32 = jnp.float32
 BF16 = jnp.bfloat16
 MESH = pl.DeviceIdType.MESH
-COPIES = 182
+COPIES = 175
 
 
 class Links:
@@ -73,13 +73,18 @@
     x, z, y, c = (lax.axis_index(a) for a in ("layer", "z", "y", "col"))
     place = {"layer": x, "z": z, "y": y, "col": c}
     links = Links(place, send_sems, recv_sems)
-    load_rows = pltpu.make_async_copy(
-        density.at[pl.ds(pl.multiple_of(x * BS, BS), BS), :], rows_in, in_sems.at[0]
+    subs = [lax.rem(x + n, 4) for n in range(4)]
+    load_rows = [
+        pltpu.make_async_copy(
+            density.at[pl.ds(pl.multiple_of(subs[n] * BS, BS), BS), :], rows_in.at[n], in_sems.at[n]
+        )
+        for n in range(2)
+    ]
+    load_cols = pltpu.make_async_copy(
+        density.at[:, pl.ds(pl.multiple_of(x * 1024, 1024), 1024)], cols_in, in_sems.at[7]
     )
-    load_cols = pltpu.make_async_copy(
-        density.at[:, pl.ds(pl.multiple_of(x * 1024, 1024), 1024)], cols_in, in_sems.at[1]
-    )
-    load_rows.start()
+    for made in load_rows:
+        made.start()
     load_cols.start()
     load_own = [
         pltpu.make_async_copy(
@@ -93,8 +98,9 @@
     load_der = pltpu.make_async_copy(derivative, der, in_sems.at[2])
     load_der.start()
     barrier = pltpu.get_barrier_semaphore()
-    others = [(dz, dy, dc) for dz in (2, 1, 3, 0) for dy in (2, 1, 3, 0) for dc in (0, 1)][:-2]
-    others.append((0, 0, 1))
+    hops = (0, 1, 2, 1)
+    others = [(dz, dy, dc) for dz in range(4) for dy in range(4) for dc in range(2)][1:]
+    others.sort(key=lambda d: -hops[d[0]] - hops[d[1]])
 
     def device(dz, dy, dc):
         return {"z": lax.rem(z + dz, 4), "y": lax.rem(y + dy, 4), "col": lax.rem(c + dc, 2)}
@@ -129,21 +135,29 @@
         inside = pattern[row_block, col_block] == 1
         return inside | ((z * 4 + y) * 4 + row_block == c * 32 + col_block)
 
-    load_rows.wait()
-    for b in range(32):
-        block = rows_in[:, b * BS : (b + 1) * BS]
-        block = jnp.where(kept(x, b), block, jnp.zeros_like(block))
-        lane = (b // 16) * 512 + (b % 4) * BS
-        left_send[(b % 16) // 4, :, lane : lane + BS] = block
-    pl.semaphore_wait(barrier, len(greeted))
-
     def over(step):
         return lax.rem(y + step, 4)
 
-    brought = {
-        step: links.copy(left_send.at[over(-step % 4)], left.at[c, y, x], "y", -step)
-        for step in (3, 1, 2)
-    }
+    brought = {}
+
+    def bring(step, n):
+        brought[step, n] = links.copy(
+            left_send.at[n, over(-step % 4)], left.at[c, y, subs[n]], "y", -step
+        )
+
+    for n in range(2):
+        load_rows[n].wait()
+        for b in range(32):
+            block = rows_in[n, :, b * BS : (b + 1) * BS]
+            block = jnp.where(kept(subs[n], b), block, jnp.zeros_like(block))
+            lane = (b // 16) * 512 + (b % 4) * BS
+            left_send[n, (b % 16) // 4, :, lane : lane + BS] = block
+        if n == 0:
+            pl.semaphore_wait(barrier, len(greeted))
+        bring(3, n)
+        bring(1, n)
+    bring(2, 0)
+    bring(2, 1)
 
     load_cols.wait()
     for b in range(8):
@@ -156,8 +170,10 @@
     for d in others:
         at = device(*d)
         requests.append(links.to(asked_send.at[holder_of(at)], asked_recv.at[me], at))
-    rights = [Ring(links, "z", lambda s, j=j: right.at[j, s]) for j in range(CHUNKS)]
-    rights[0].start()
+    rights = [
+        [links.copy(right.at[j, z], right.at[j, z], "z", step) for step in (1, -1, 2)]
+        for j in range(CHUNKS)
+    ]
 
     for made in load_own:
         made.wait()
@@ -169,26 +185,21 @@
                 lane = h * 512 + w * BS
                 left[c, y, r, :, lane : lane + BS] = block
     crossed = {0: [links.copy(left.at[c, y], left.at[c, y], "col", 1)], 1: [], 2: [], 3: []}
-    lefts = {}
+    passed = {}
 
     def cross(step, away):
-        piece = left.at[c, over(step), lax.rem(x + away, 4)]
+        piece = left.at[c, over(step), subs[away]]
         crossed[step].append(links.copy(piece, piece, "col", 1))
 
-    def spread(step):
-        brought[step].wait_recv()
-        lefts[step] = Ring(links, "layer", lambda s: left.at[c, over(step), s])
-        lefts[step].start()
-        cross(step, 0)
-
-    def relay(step):
-        lefts[step].forward()
-        cross(step, 3)
-        cross(step, 1)
-
-    def gathered(step):
-        lefts[step].finish()
-        cross(step, 2)
+    def spread(step, n):
+        brought[step, n].wait_recv()
+        piece = left.at[c, over(step), subs[n]]
+        passed[step, n] = links.copy(piece, piece, "layer", 1 - 2 * n)
+        cross(step, n)
+
+    def took(step, n):
+        passed[step, n].wait_recv()
+        cross(step, 3 - n)
 
     def complete(*steps):
         for step in steps:
@@ -281,13 +292,19 @@
         for b in range(2):
             held[where + b] = pure[j, x, b]
 
-    spread(3)
-    spread(1)
-    rights[0].forward()
-    rights[1].start()
-    spread(2)
-    relay(3)
-    relay(1)
+    def righted(j):
+        for made in rights[j]:
+            made.wait_recv()
+
+    spread(3, 0)
+    spread(1, 0)
+    spread(3, 1)
+    spread(1, 1)
+    took(3, 0)
+    spread(2, 0)
+    took(3, 1)
+    took(1, 0)
+    spread(2, 1)
     for made in requests:
         made.wait_recv()
     asked_rows[...] = asked_recv[:, 0, :]
@@ -297,52 +314,48 @@
     ]
     for made in tables:
         made.start()
-    gathered(3)
-    gathered(1)
-    rights[1].forward()
-    rights[2].start()
-    relay(2)
+    took(1, 1)
+    took(2, 0)
     for made in tables:
         made.wait()
-    rights[0].finish()
+    righted(0)
     complete(0, 3, 1)
     squares[0].near(right)
-    gathered(2)
-    rights[1].finish()
+    righted(1)
     squares[1].near(right)
-    rights[2].forward()
-    rights[3].start()
+    took(2, 1)
     complete(2)
     squares[0].far(right)
     squares[1].far(right)
+    righted(2)
+    squares[2].near(right)
     squares[0].combine()
-    rights[2].finish()
     squares[2].far(right)
-    squares[2].near(right)
     squares[1].combine()
     squared(0)
-    rights[3].forward()
-    rights[3].finish()
-    squares[3].far(right)
+    righted(3)
     squares[3].near(right)
     squares[2].combine()
+    squares[3].far(right)
     squared(1)
     gathers[0].forward()
+    squared(2)
+    gathers[1].forward()
     squares[3].combine()
     second(0)
-    squared(2)
-    gathers[1].forward()
+    squared(3)
     cubes[0].combine()
+    gathers[2].forward()
     second(1)
-    squared(3)
-    gathers[2].forward()
+    purified(0)
     cubes[1].combine()
-    purified(0)
+    gathers[3].forward()
     second(2)
-    gathers[3].forward()
+    purified(1)
+    gathers[3].finish()
+    cubes[3].far(square)
     cubes[2].combine()
-    purified(1)
-    second(3)
+    cubes[3].near(square)
     cubes[3].combine()
     purified(2)
     purified(3)
@@ -393,11 +406,11 @@
         in_specs=[pl.BlockSpec(memory_space=pltpu.SMEM), hbm, vmem, vmem, vmem, hbm],
         out_specs=vmem,
         scratch_shapes=[
-            pltpu.VMEM((BS, 4096), BF16),
+            pltpu.VMEM((2, BS, 4096), BF16),
             pltpu.VMEM((512, 1024), BF16),
             pltpu.VMEM((2, 512, 512), BF16),
             pltpu.VMEM((2, 4, 4, BS, 1024), BF16),
-            pltpu.VMEM((4, BS, 1024), BF16),
+            pltpu.VMEM((2, 4, BS, 1024), BF16),
             pltpu.VMEM((CHUNKS, 4, 512, WIDE), BF16),
             pltpu.VMEM((CHUNKS, 4, 512, WIDE), BF16),
             pltpu.VMEM((CHUNKS, 4, 512, WIDE), F32),
@@ -415,7 +428,7 @@
             pltpu.VMEM((32, 2, BS, BS), BF16),
             pltpu.VMEM((64, BS, BS), BF16),
             pltpu.VMEM((3, 32, 8, BS), F32),
-            pltpu.SemaphoreType.DMA((7,)),
+            pltpu.SemaphoreType.DMA((8,)),
             pltpu.SemaphoreType.DMA((COPIES,)),
             pltpu.SemaphoreType.DMA((COPIES,)),
         ],

time: 159 us -> 153 us (0.962)
  Pallas kernels: 157 us -> 152 us
    pallas_call x1, Pallas kernels: 157 us -> 152 us  [shards(): pl.pallas_call(purify_kernel, out_shape=jax.ShapeDtypeStruct((3, ATOM_DEV...]
where the time goes in v5:
time: 153 us
  Pallas kernels  152 us (99%)
    pallas_call x1, Pallas kernels, shards(): pl.pallas_call(purify_kernel, out_shape=jax.ShapeDtypeStruct((3, ATOM_DEV...  152 us

profile of v5, /device:TPU:1, one launch (start us, length us, event | category | flops | bytes accessed | tf_op | source)
XLA Modules:
  0.0 153.3 jit_solution(6469477487974135922)
XLA Ops:
  0.0 152.0 %shard_map.64 = f32[3,8]{1,0:T(4,128)} custom-call(s32[4,32]{1,0:T(4,128)} %pattern.1, bf16[512,4096]{1,0:T(8,128)(2,1)} %density.1, s32[1,32]{1,0:T(1,128)} %bitcast.3, s32[1,32]{1,0:T(1,128)} %bitcast.4, s32[1,32]{1,0:T(1,128)} %bitcast.5, bf16[32,3,128,128]{3,2,1,0:T(8,128)(2,1)} %derivative.1), custom_call_target="tpu_custom_call" | custom-call | tf_op jit(solution)/shard_map/pallas_call | solution.py:403
  152.0 1.3 copy.8

commit v6 on v5

--- a/solution.py
+++ b/solution.py
@@ -109,7 +109,9 @@
         return at["z"] * 8 + at["y"] * 2 + at["col"]
 
     me = z * 8 + y * 2 + c
-    greeted = [device(*d) for d in others] + [{"layer": lax.rem(x + step, 4)} for step in (1, 2, 3)]
+    greeted = [{"col": 1 - c}]
+    for axis in ("y", "z", "layer"):
+        greeted += [{axis: lax.rem(place[axis] + step, 4)} for step in (1, 2, 3)]
     for at in greeted:
         pl.semaphore_signal(barrier, inc=1, device_id=at, device_id_type=MESH)
 
@@ -166,10 +168,6 @@
             block = jnp.where(kept(r, x * 8 + b), block, jnp.zeros_like(block))
             lane = (b % 2) * BS
             right[b // 2, z, r * BS : (r + 1) * BS, lane : lane + BS] = block
-    requests = []
-    for d in others:
-        at = device(*d)
-        requests.append(links.to(asked_send.at[holder_of(at)], asked_recv.at[me], at))
     rights = [
         [links.copy(right.at[j, z], right.at[j, z], "z", step) for step in (1, -1, 2)]
         for j in range(CHUNKS)
@@ -305,19 +303,8 @@
     took(3, 1)
     took(1, 0)
     spread(2, 1)
-    for made in requests:
-        made.wait_recv()
-    asked_rows[...] = asked_recv[:, 0, :]
-    tables = [
-        pltpu.make_async_copy(asked_rows, asked, in_sems.at[3]),
-        pltpu.make_async_copy(spots, spot_of, in_sems.at[4]),
-    ]
-    for made in tables:
-        made.start()
     took(1, 1)
     took(2, 0)
-    for made in tables:
-        made.wait()
     righted(0)
     complete(0, 3, 1)
     squares[0].near(right)
@@ -333,6 +320,10 @@
     squares[2].far(right)
     squares[1].combine()
     squared(0)
+    requests = []
+    for d in others:
+        at = device(*d)
+        requests.append(links.to(asked_send.at[holder_of(at)], asked_recv.at[me], at))
     righted(3)
     squares[3].near(right)
     squares[2].combine()
@@ -347,6 +338,15 @@
     cubes[0].combine()
     gathers[2].forward()
     second(1)
+    for made in requests:
+        made.wait_recv()
+    asked_rows[...] = asked_recv[:, 0, :]
+    tables = [
+        pltpu.make_async_copy(asked_rows, asked, in_sems.at[3]),
+        pltpu.make_async_copy(spots, spot_of, in_sems.at[4]),
+    ]
+    for made in tables:
+        made.start()
     purified(0)
     cubes[1].combine()
     gathers[3].forward()
@@ -361,6 +361,8 @@
     purified(3)
     for made in handed:
         made.wait_recv()
+    for made in tables:
+        made.wait()
     fetches = []
     for d in others:
         at = device(*d)

time: 153 us -> 155 us (1.013); the launches traced: 153 us -> 152 us
  Pallas kernels: 152 us -> 150 us
    pallas_call x1, Pallas kernels: 152 us -> 150 us  [shards(): pl.pallas_call(purify_kernel, out_shape=jax.ShapeDtypeStruct((3, ATOM_DEV...]
where the time goes in v6:
time: 155 us; the launch traced here: 152 us
  Pallas kernels  150 us (97%)
    pallas_call x1, Pallas kernels, shards(): pl.pallas_call(purify_kernel, out_shape=jax.ShapeDtypeStruct((3, ATOM_DEV...  150 us

profile of v6, /device:TPU:1, one launch (start us, length us, event | category | flops | bytes accessed | tf_op | source)
XLA Modules:
  0.0 151.7 jit_solution(436788295885259277)
XLA Ops:
  0.0 150.4 %shard_map.64 = f32[3,8]{1,0:T(4,128)} custom-call(s32[4,32]{1,0:T(4,128)} %pattern.1, bf16[512,4096]{1,0:T(8,128)(2,1)} %density.1, s32[1,32]{1,0:T(1,128)} %bitcast.3, s32[1,32]{1,0:T(1,128)} %bitcast.4, s32[1,32]{1,0:T(1,128)} %bitcast.5, bf16[32,3,128,128]{3,2,1,0:T(8,128)(2,1)} %derivative.1), custom_call_target="tpu_custom_call" | custom-call | tf_op jit(solution)/shard_map/pallas_call | solution.py:405
  150.4 1.3 copy.8

commit v7 on v5

--- a/solution.py
+++ b/solution.py
@@ -12,7 +12,7 @@
 F32 = jnp.float32
 BF16 = jnp.bfloat16
 MESH = pl.DeviceIdType.MESH
-COPIES = 175
+COPIES = 242
 
 
 class Links:
@@ -66,10 +66,11 @@
 
 def purify_kernel(
     pattern, density, targets_row, slots_row, atoms_row, derivative, forces,
-    rows_in, cols_in, own_in, left, left_send, right, square, part, sums_send, sums_recv, pure, held,
-    der, asked_send, asked_recv, asked_rows, spots, asked, spot_of, picked, arrived, contrib,
+    rows_in, cols_in, own_in, left, left_send, right, square, part, sums_send, sums_recv, cube_send, cube_recv, pure, held_low, held_high,
+    der, asked_send, asked_recv, asked_rows, spots, asked, spot_of, picked, arrived_low, arrived_high, contrib,
     in_sems, send_sems, recv_sems,
 ):
+    held, arrived = (held_low, held_high), (arrived_low, arrived_high)
     x, z, y, c = (lax.axis_index(a) for a in ("layer", "z", "y", "col"))
     place = {"layer": x, "z": z, "y": y, "col": c}
     links = Links(place, send_sems, recv_sems)
@@ -206,91 +207,142 @@
             for made in crossed[step]:
                 made.wait_recv()
 
-    def multiply(j, factor, panels):
+    def multiply(j, factor, panels, half):
+        height = 512 if half is None else 256
+        base = 256 * (half or 0)
+
         def panel(turn, carry):
             i = jnp.where(turn == 0, panels[0], panels[1])
             d = lax.rem(y + jnp.where(i == 0, 2, jnp.where(i == 1, 1, jnp.where(i == 2, 3, 0))), 4)
-            total = jnp.zeros((512, WIDE), F32)
+            total = jnp.zeros((height, WIDE), F32)
             for k in range(2):
+                if half is None:
+                    rows = left[k, d]
+                else:
+                    rows = left[k, d, :, 64 * half : 64 * half + 64, :]
                 total += jnp.dot(
-                    left[k, d].reshape(512, 1024),
+                    rows.reshape(height, 1024),
                     factor[j, 2 * k : 2 * k + 2].reshape(1024, WIDE),
                     preferred_element_type=F32,
                 )
-            part[j, i] = total
+            part[j, i, base : base + height] = total
             return carry
 
         lax.fori_loop(0, 2, panel, 0)
 
     class Sums:
-        def __init__(self, j, stage):
-            self.j, self.slot, self.made = j, stage * CHUNKS + j, {}
+        def __init__(self, j, half, factor, sent, received):
+            self.j, self.half, self.factor = j, half, factor
+            self.sent, self.received, self.made = sent, received, {}
+            self.low = 256 * (half or 0)
+            self.size = 256 if half is None else 128
+
+        def own(self, i, upper):
+            start = self.low + self.size * upper
+            return part[self.j, i, start : start + self.size]
 
         def send(self, n, value, step):
-            sums_send[self.slot, n] = value.astype(BF16)
-            return links.copy(sums_send.at[self.slot, n], sums_recv.at[self.slot, n], "y", step)
-
-        def far(self, factor):
-            j = self.j
-            multiply(j, factor, (0, 3))
-            self.made[0] = self.send(0, part[j, 0, 0:256], 1)
-            self.made[1] = self.send(1, part[j, 0, 256:512], -1)
-
-        def near(self, factor):
-            j = self.j
-            multiply(j, factor, (1, 2))
-            self.made[2] = self.send(2, part[j, 1, 256:512], 1)
-            self.made[3] = self.send(3, part[j, 2, 0:256], -1)
+            self.sent[n] = value.astype(BF16)
+            self.made[n] = links.copy(self.sent.at[n], self.received.at[n], "y", step)
+
+        def far(self):
+            multiply(self.j, self.factor, (0, 3), self.half)
+            self.send(0, self.own(0, 0), 1)
+            self.send(1, self.own(0, 1), -1)
+
+        def near(self):
+            multiply(self.j, self.factor, (1, 2), self.half)
+            self.send(2, self.own(1, 1), 1)
+            self.send(3, self.own(2, 0), -1)
 
         def combine(self):
-            j = self.j
             self.made[0].wait_recv()
-            self.made[4] = self.send(4, part[j, 1, 0:256] + sums_recv[self.slot, 0].astype(F32), 1)
+            self.send(4, self.own(1, 0) + self.received[0].astype(F32), 1)
             self.made[1].wait_recv()
-            self.made[5] = self.send(5, part[j, 2, 256:512] + sums_recv[self.slot, 1].astype(F32), -1)
+            self.send(5, self.own(2, 1) + self.received[1].astype(F32), -1)
 
         def result(self):
             for n in (2, 3, 4, 5):
                 self.made[n].wait_recv()
-            halves = []
-            for h, (a, b) in enumerate(((3, 4), (2, 5))):
-                own = part[self.j, 3, h * 256 : (h + 1) * 256]
-                halves.append(
-                    own + sums_recv[self.slot, a].astype(F32) + sums_recv[self.slot, b].astype(F32)
-                )
-            return halves
-
-    squares = [Sums(j, 0) for j in range(CHUNKS)]
-    cubes = [Sums(j, 1) for j in range(CHUNKS)]
+            return [
+                self.own(3, h) + self.received[a].astype(F32) + self.received[b].astype(F32)
+                for h, (a, b) in enumerate(((3, 4), (2, 5)))
+            ]
+
+    squares = [Sums(j, None, right, sums_send.at[j], sums_recv.at[j]) for j in range(CHUNKS)]
+    cubes = [
+        [
+            Sums(j, half, square, cube_send.at[half, j], cube_recv.at[half, j])
+            for j in range(CHUNKS)
+        ]
+        for half in range(2)
+    ]
     gathers = [Ring(links, "z", lambda s, j=j: square.at[j, s]) for j in range(CHUNKS)]
-    handed = []
+    handed = [[], []]
 
     def squared(j):
         for h, value in enumerate(squares[j].result()):
             square[j, z, h * 256 : (h + 1) * 256] = value.astype(BF16)
         gathers[j].start()
 
-    def second(j):
-        gathers[j].finish()
-        cubes[j].far(square)
-        cubes[j].near(square)
-
-    def purified(j):
-        for h, value in enumerate(cubes[j].result()):
+    gone = set()
+
+    def second(half, j):
+        if j not in gone:
+            gathers[j].finish()
+            gone.add(j)
+        cubes[half][j].far()
+        cubes[half][j].near()
+
+    def purified(half, j):
+        for h, value in enumerate(cubes[half][j].result()):
             for r in range(2):
                 row = 2 * h + r
+                start = row * BS + 64 * half
                 for b in range(2):
                     lanes = slice(b * BS, (b + 1) * BS)
-                    own = square[j, z, row * BS : (row + 1) * BS, lanes].astype(F32)
-                    block = 3.0 * own - 2.0 * value[r * BS : (r + 1) * BS, lanes]
+                    own = square[j, z, start : start + 64, lanes].astype(F32)
+                    block = 3.0 * own - 2.0 * value[64 * r : 64 * r + 64, lanes]
                     block = jnp.where(kept(row, x * 8 + j * 2 + b), block, jnp.zeros_like(block))
-                    pure[j, row, b] = block.astype(BF16)
+                    pure[half, j, row, b] = block.astype(BF16)
         where = x * 8 + j * 2
         for step in (1, 2, 3):
             to = lax.rem(x + step, 4)
-            handed.append(links.copy(pure.at[j, to], held.at[pl.ds(where, 2)], "layer", step))
+            handed[half].append(
+                links.copy(pure.at[half, j, to], held[half].at[pl.ds(where, 2)], "layer", step)
+            )
         for b in range(2):
-            held[where + b] = pure[j, x, b]
+            held[half][where + b] = pure[half, j, x, b]
+
+    fetches = [[], []]
+
+    def fetch(half):
+        for made in handed[half]:
+            made.wait_recv()
+        for d in others:
+            at = device(*d)
+            to = holder_of(at)
+            for k in range(2):
+                picked[half, to, k] = held[half][asked[to, k]]
+            fetches[half].append(
+                links.to(picked.at[half, to], arrived[half].at[pl.ds(2 * me, 2)], at)
+            )
+        for k in range(2):
+            arrived[half][2 * me + k] = held[half][asked[me, k]]
+
+    def contract(half):
+        for made in fetches[half]:
+            made.wait_recv()
+
+        def entry(e, carry):
+            block = arrived[half][spot_of[0, e]].astype(F32)
+            for k in range(3):
+                terms = block * der[e, k, 64 * half : 64 * half + 64, :].astype(F32)
+                total = jnp.sum(terms.reshape(8, 8, BS), axis=0)
+                contrib[k, e] = total if half == 0 else contrib[k, e] + total
+            return carry
+
+        lax.fori_loop(0, 32, entry, 0)
 
     def righted(j):
         for made in rights[j]:
@@ -318,70 +370,61 @@
     took(2, 0)
     for made in tables:
         made.wait()
-    righted(0)
     complete(0, 3, 1)
-    squares[0].near(right)
-    righted(1)
-    squares[1].near(right)
+    for j in (0, 1):
+        righted(j)
+        squares[j].near()
     took(2, 1)
     complete(2)
-    squares[0].far(right)
-    squares[1].far(right)
+    squares[0].far()
+    squares[1].far()
+    squares[0].combine()
+    squares[1].combine()
     righted(2)
-    squares[2].near(right)
-    squares[0].combine()
-    squares[2].far(right)
-    squares[1].combine()
+    squares[2].near()
+    squares[2].far()
     squared(0)
+    squared(1)
     righted(3)
-    squares[3].near(right)
+    squares[3].near()
+    squares[3].far()
     squares[2].combine()
-    squares[3].far(right)
-    squared(1)
     gathers[0].forward()
+    squares[3].combine()
+    gathers[1].forward()
     squared(2)
-    gathers[1].forward()
-    squares[3].combine()
-    second(0)
+    second(0, 0)
+    cubes[0][0].combine()
+    second(1, 0)
     squared(3)
-    cubes[0].combine()
+    second(0, 1)
+    cubes[1][0].combine()
     gathers[2].forward()
-    second(1)
-    purified(0)
-    cubes[1].combine()
+    second(1, 1)
+    cubes[0][1].combine()
+    purified(0, 0)
+    purified(1, 0)
     gathers[3].forward()
-    second(2)
-    purified(1)
-    gathers[3].finish()
-    cubes[3].far(square)
-    cubes[2].combine()
-    cubes[3].near(square)
-    cubes[3].combine()
-    purified(2)
-    purified(3)
-    for made in handed:
-        made.wait_recv()
-    fetches = []
-    for d in others:
-        at = device(*d)
-        to = holder_of(at)
-        for k in range(2):
-            picked[to, k] = held[asked[to, k]]
-        fetches.append(links.to(picked.at[to], arrived.at[pl.ds(2 * me, 2)], at))
-    for k in range(2):
-        arrived[2 * me + k] = held[asked[me, k]]
+    cubes[1][1].combine()
+    second(0, 2)
+    purified(0, 1)
+    second(0, 3)
+    purified(1, 1)
+    cubes[0][2].combine()
+    cubes[0][3].combine()
+    second(1, 2)
+    second(1, 3)
+    purified(0, 2)
+    purified(0, 3)
+    cubes[1][2].combine()
+    cubes[1][3].combine()
+    fetch(0)
+    purified(1, 2)
+    purified(1, 3)
     load_der.wait()
-    for made in fetches:
-        made.wait_recv()
-
-    def contract(e, carry):
-        block = arrived[spot_of[0, e]].astype(F32)
-        for k in range(3):
-            terms = block * der[e, k].astype(F32)
-            contrib[k, e] = jnp.sum(terms.reshape(16, 8, BS), axis=0)
-        return carry
-
-    lax.fori_loop(0, 32, contract, 0)
+    fetch(1)
+    contract(0)
+    contract(1)
     atoms = lax.broadcasted_iota(jnp.int32, (32, ATOM_DEV), 1)
     atom_hot = jnp.where(column(atoms_row[...]) == atoms, 1.0, 0.0).astype(F32)
     for k in range(3):
@@ -414,10 +457,13 @@
             pltpu.VMEM((CHUNKS, 4, 512, WIDE), BF16),
             pltpu.VMEM((CHUNKS, 4, 512, WIDE), BF16),
             pltpu.VMEM((CHUNKS, 4, 512, WIDE), F32),
-            pltpu.VMEM((2 * CHUNKS, 6, 256, WIDE), BF16),
-            pltpu.VMEM((2 * CHUNKS, 6, 256, WIDE), BF16),
-            pltpu.VMEM((CHUNKS, 4, 2, BS, BS), BF16),
-            pltpu.VMEM((32, BS, BS), BF16),
+            pltpu.VMEM((CHUNKS, 6, 256, WIDE), BF16),
+            pltpu.VMEM((CHUNKS, 6, 256, WIDE), BF16),
+            pltpu.VMEM((2, CHUNKS, 6, BS, WIDE), BF16),
+            pltpu.VMEM((2, CHUNKS, 6, BS, WIDE), BF16),
+            pltpu.VMEM((2, CHUNKS, 4, 2, 64, BS), BF16),
+            pltpu.VMEM((32, 64, BS), BF16),
+            pltpu.VMEM((32, 64, BS), BF16),
             pltpu.VMEM((32, 3, BS, BS), BF16),
             pltpu.VMEM((32, 8, BS), jnp.int32),
             pltpu.VMEM((32, 8, BS), jnp.int32),
@@ -425,8 +471,9 @@
             pltpu.VMEM((8, BS), jnp.int32),
             pltpu.SMEM((32, BS), jnp.int32),
             pltpu.SMEM((8, BS), jnp.int32),
-            pltpu.VMEM((32, 2, BS, BS), BF16),
-            pltpu.VMEM((64, BS, BS), BF16),
+            pltpu.VMEM((2, 32, 2, 64, BS), BF16),
+            pltpu.VMEM((64, 64, BS), BF16),
+            pltpu.VMEM((64, 64, BS), BF16),
             pltpu.VMEM((3, 32, 8, BS), F32),
             pltpu.SemaphoreType.DMA((8,)),
             pltpu.SemaphoreType.DMA((COPIES,)),

time: 153 us -> 146 us (0.954)
  Pallas kernels: 152 us -> 145 us
    pallas_call x1, Pallas kernels: 152 us -> 145 us  [shards(): pl.pallas_call(purify_kernel, out_shape=jax.ShapeDtypeStruct((3, ATOM_DEV...]
where the time goes in v7:
time: 146 us
  Pallas kernels  145 us (99%)
    pallas_call x1, Pallas kernels, shards(): pl.pallas_call(purify_kernel, out_shape=jax.ShapeDtypeStruct((3, ATOM_DEV...  145 us

profile of v7, /device:TPU:1, one launch (start us, length us, event | category | flops | bytes accessed | tf_op | source)
XLA Modules:
  0.0 146.1 jit_solution(6988637824118699308)
XLA Ops:
  0.0 144.9 %shard_map.64 = f32[3,8]{1,0:T(4,128)} custom-call(s32[4,32]{1,0:T(4,128)} %pattern.1, bf16[512,4096]{1,0:T(8,128)(2,1)} %density.1, s32[1,32]{1,0:T(1,128)} %bitcast.3, s32[1,32]{1,0:T(1,128)} %bitcast.4, s32[1,32]{1,0:T(1,128)} %bitcast.5, bf16[32,3,128,128]{3,2,1,0:T(8,128)(2,1)} %derivative.1), custom_call_target="tpu_custom_call" | custom-call | tf_op jit(solution)/shard_map/pallas_call | solution.py:446
  144.9 1.3 copy.8

commit v8 on v7

--- a/solution.py
+++ b/solution.py
@@ -342,7 +342,7 @@
                 contrib[k, e] = total if half == 0 else contrib[k, e] + total
             return carry
 
-        lax.fori_loop(0, 32, entry, 0)
+        lax.fori_loop(0, 32, entry, 0, unroll=4)
 
     def righted(j):
         for made in rights[j]:
@@ -418,8 +418,8 @@
     purified(0, 3)
     cubes[1][2].combine()
     cubes[1][3].combine()
+    purified(1, 2)
     fetch(0)
-    purified(1, 2)
     purified(1, 3)
     load_der.wait()
     fetch(1)
@@ -428,13 +428,8 @@
     atoms = lax.broadcasted_iota(jnp.int32, (32, ATOM_DEV), 1)
     atom_hot = jnp.where(column(atoms_row[...]) == atoms, 1.0, 0.0).astype(F32)
     for k in range(3):
-        lanes = jnp.sum(contrib[k], axis=1)
-        terms = lax.dot_general(
-            jnp.ones((8, BS), F32), lanes, (((1,), (1,)), ((), ())),
-            precision=lax.Precision.HIGHEST, preferred_element_type=F32,
-        )
-        summed = jnp.dot(terms, atom_hot, precision=lax.Precision.HIGHEST, preferred_element_type=F32)
-        forces[k : k + 1, :] = -2.0 * summed[0:1, :]
+        terms = jnp.sum(jnp.sum(contrib[k], axis=1), axis=1, keepdims=True)
+        forces[k : k + 1, :] = -2.0 * jnp.sum(terms * atom_hot, axis=0, keepdims=True)
     for made in links.started:
         made.wait_send()
     assert links.count == COPIES, links.count

time: 146 us -> 146 us (level)
  no operation moved by 1% of the time
where the time goes in v8:
time: 146 us; the launch traced here: 145 us
  Pallas kernels  144 us (99%)
    pallas_call x1, Pallas kernels, shards(): pl.pallas_call(purify_kernel, out_shape=jax.ShapeDtypeStruct((3, ATOM_DEV...  144 us

profile of v8, /device:TPU:1, one launch (start us, length us, event | category | flops | bytes accessed | tf_op | source)
XLA Modules:
  0.0 145.4 jit_solution(13105724731576311540)
XLA Ops:
  0.0 144.1 %shard_map.64 = f32[3,8]{1,0:T(4,128)} custom-call(s32[4,32]{1,0:T(4,128)} %pattern.1, bf16[512,4096]{1,0:T(8,128)(2,1)} %density.1, s32[1,32]{1,0:T(1,128)} %bitcast.3, s32[1,32]{1,0:T(1,128)} %bitcast.4, s32[1,32]{1,0:T(1,128)} %bitcast.5, bf16[32,3,128,128]{3,2,1,0:T(8,128)(2,1)} %derivative.1), custom_call_target="tpu_custom_call" | custom-call | tf_op jit(solution)/shard_map/pallas_call | solution.py:441
  144.1 1.3 copy.8

commit v9 on v8

--- a/solution.py
+++ b/solution.py
@@ -110,7 +110,9 @@
         return at["z"] * 8 + at["y"] * 2 + at["col"]
 
     me = z * 8 + y * 2 + c
-    greeted = [device(*d) for d in others] + [{"layer": lax.rem(x + step, 4)} for step in (1, 2, 3)]
+    greeted = [{"col": 1 - c}]
+    for axis in ("y", "z", "layer"):
+        greeted += [{axis: lax.rem(place[axis] + step, 4)} for step in (1, 2, 3)]
     for at in greeted:
         pl.semaphore_signal(barrier, inc=1, device_id=at, device_id_type=MESH)
 
@@ -167,10 +169,6 @@
             block = jnp.where(kept(r, x * 8 + b), block, jnp.zeros_like(block))
             lane = (b % 2) * BS
             right[b // 2, z, r * BS : (r + 1) * BS, lane : lane + BS] = block
-    requests = []
-    for d in others:
-        at = device(*d)
-        requests.append(links.to(asked_send.at[holder_of(at)], asked_recv.at[me], at))
     rights = [
         [links.copy(right.at[j, z], right.at[j, z], "z", step) for step in (1, -1, 2)]
         for j in range(CHUNKS)
@@ -357,19 +355,8 @@
     took(3, 1)
     took(1, 0)
     spread(2, 1)
-    for made in requests:
-        made.wait_recv()
-    asked_rows[...] = asked_recv[:, 0, :]
-    tables = [
-        pltpu.make_async_copy(asked_rows, asked, in_sems.at[3]),
-        pltpu.make_async_copy(spots, spot_of, in_sems.at[4]),
-    ]
-    for made in tables:
-        made.start()
     took(1, 1)
     took(2, 0)
-    for made in tables:
-        made.wait()
     complete(0, 3, 1)
     for j in (0, 1):
         righted(j)
@@ -384,6 +371,10 @@
     squares[2].near()
     squares[2].far()
     squared(0)
+    requests = []
+    for d in others:
+        at = device(*d)
+        requests.append(links.to(asked_send.at[holder_of(at)], asked_recv.at[me], at))
     squared(1)
     righted(3)
     squares[3].near()
@@ -414,11 +405,22 @@
     cubes[0][3].combine()
     second(1, 2)
     second(1, 3)
+    for made in requests:
+        made.wait_recv()
+    asked_rows[...] = asked_recv[:, 0, :]
+    tables = [
+        pltpu.make_async_copy(asked_rows, asked, in_sems.at[3]),
+        pltpu.make_async_copy(spots, spot_of, in_sems.at[4]),
+    ]
+    for made in tables:
+        made.start()
     purified(0, 2)
     purified(0, 3)
     cubes[1][2].combine()
     cubes[1][3].combine()
     purified(1, 2)
+    for made in tables:
+        made.wait()
     fetch(0)
     purified(1, 3)
     load_der.wait()

time: 146 us -> 144 us (0.986)
  no operation moved by 1% of the time
where the time goes in v9:
time: 144 us
  Pallas kernels  143 us (99%)
    pallas_call x1, Pallas kernels, shards(): pl.pallas_call(purify_kernel, out_shape=jax.ShapeDtypeStruct((3, ATOM_DEV...  143 us

profile of v9, /device:TPU:1, one launch (start us, length us, event | category | flops | bytes accessed | tf_op | source)
XLA Modules:
  0.0 144.0 jit_solution(2533515429733495848)
XLA Ops:
  0.0 142.7 %shard_map.64 = f32[3,8]{1,0:T(4,128)} custom-call(s32[4,32]{1,0:T(4,128)} %pattern.1, bf16[512,4096]{1,0:T(8,128)(2,1)} %density.1, s32[1,32]{1,0:T(1,128)} %bitcast.3, s32[1,32]{1,0:T(1,128)} %bitcast.4, s32[1,32]{1,0:T(1,128)} %bitcast.5, bf16[32,3,128,128]{3,2,1,0:T(8,128)(2,1)} %derivative.1), custom_call_target="tpu_custom_call" | custom-call | tf_op jit(solution)/shard_map/pallas_call | solution.py:443
  142.7 1.3 copy.8
